TPU v7x, 32 devices: a whole 2x2x4 slice. The times are simulated.
32 devices in a mesh: freq: 4 (over y, x), param: 8 (over z, core).
Axes of the slice: x: 2, y: 2, z: 4, core: 2. Of those that a mesh axis runs over, the one named last changes fastest.
Arguments:
- chain_state: float32 [32, 2048, 512], P('freq', 'param'), may hold values from -6 to 6
- second_moment: float32 [32, 2048, 512], P('freq', 'param'), may hold values from 0.25 to 2
- noise: float32 [2, 32, 2048, 512], P(None, 'freq', 'param'), may hold values from -6 to 6
- green: bfloat16 [2, 64, 2048, 512], P(None, 'freq', 'param'), may hold values from -0.125 to 0.125
- observed: float32 [64, 1024], P('freq'), may hold values from -6 to 6
- inv_noise: float32 [64, 512], P('freq'), may hold values from 0.3 to 3
- temper: float32 [32], P('freq'), may hold values from 0.2 to 1
Outputs:
- new_state: float32 [32, 2048, 512], P('freq', 'param')
- new_moment: float32 [32, 2048, 512], P('freq', 'param')
All inputs are finite; a program needn't handle non-finite values.
Results may differ from a plain program's by a relative error of at most 0.005.
Values may be sent and summed in bfloat16 or wider, within the bound.
A program may use at most 128 MiB of HBM per device.

v0:
```python
import functools
import math

import jax
import jax.numpy as jnp
from jax import lax
from jax.experimental import pallas as pl
from jax.experimental.pallas import tpu as pltpu
from jax.sharding import PartitionSpec as P

decay_rate = 0.9
step_length = 0.5
MESH = pl.DeviceIdType.MESH
LANES = 128
CHUNK_FREQS = 2
STAGE_TICKS = (0, 1, 3, 5, 7, 9, 10)


def spectral_table(time_len, freq_total):
    time_index = jnp.arange(time_len, dtype=jnp.int32)[:, None]
    wave_number = jnp.arange(freq_total, dtype=jnp.int32)[None, :] + 1
    phase_angle = (time_index * wave_number % time_len).astype(jnp.float32) * (
        2.0 * math.pi / time_len
    )
    columns_table = jnp.stack([jnp.cos(phase_angle), -jnp.sin(phase_angle)], axis=-1).reshape(
        time_len, 2 * freq_total
    )
    return (columns_table / math.sqrt(time_len)).astype(jnp.bfloat16)


def exchange_kernel(
    freq_count, chunk_freqs, stage_ticks,
    spec_ref, green_hbm, obs_ref, inv_ref, own_ref,
    obs_blocks, inv_blocks, green, field, acc, outgoing, incoming, wtd, adj,
    green_sem, spec_send, spec_recv, line_send, line_recv, adj_send, adj_recv, local_sem,
):
    freq_me = lax.axis_index("freq")
    param_me = lax.axis_index("param")
    freq_loc, rows = spec_ref.shape[1], spec_ref.shape[2]
    half_rows = rows // 2
    sensors = green.shape[3]
    col_blocks = sensors // LANES
    chunk_blocks = chunk_freqs * col_blocks
    chunks = freq_loc // chunk_freqs
    core = lax.rem(param_me, 2)
    chip = param_me // 2
    side = chip // 2
    outer = (chip + side) % 2 == 0
    inner = (chip + side) % 2 == 1
    core_peer = param_me + 1 - 2 * core
    chip_peer = param_me + 2 * (1 - 2 * lax.rem(chip, 2))
    mid_peer = param_me + 2 * (1 - 2 * side)
    core_len, mid_len = chunk_blocks // 2, chunk_blocks // 4
    core_off = core * core_len
    mid_off = core_off + side * mid_len

    def freq_peer(d):
        return lax.rem(freq_me + d, freq_count)

    def freq_source(d):
        return lax.rem(freq_me + freq_count - d, freq_count)

    barrier = pltpu.get_barrier_semaphore()
    for d in range(1, freq_count):
        pl.semaphore_signal(barrier, inc=1, device_id={"freq": freq_peer(d)}, device_id_type=MESH)
    for peer in (core_peer, chip_peer):
        pl.semaphore_signal(barrier, inc=1, device_id={"param": peer}, device_id_type=MESH)

    @pl.when(inner)
    def _():
        pl.semaphore_signal(barrier, inc=1, device_id={"param": mid_peer}, device_id_type=MESH)

    def green_copy(i):
        part = pl.ds(i * chunk_freqs, chunk_freqs)
        return pltpu.make_async_copy(green_hbm.at[:, part], green.at[:, part], green_sem.at[i])

    def own_spec_copy():
        return pltpu.make_async_copy(spec_ref.at[freq_me], field.at[:, freq_me], local_sem.at[0])

    def spec_copy(i, d):
        part = pl.ds(i * chunk_freqs, chunk_freqs)
        return pltpu.make_async_remote_copy(
            src_ref=spec_ref.at[freq_peer(d), part],
            dst_ref=field.at[part, freq_me],
            send_sem=spec_send.at[d - 1, i],
            recv_sem=spec_recv.at[d - 1, i],
            device_id={"freq": freq_peer(d)},
            device_id_type=MESH,
        )

    def param_copy(k, i, src, dst, peer):
        return pltpu.make_async_remote_copy(
            src_ref=src,
            dst_ref=dst,
            send_sem=line_send.at[k, i],
            recv_sem=line_recv.at[k, i],
            device_id={"param": peer},
            device_id_type=MESH,
        )

    def core_reduce(i):
        src = outgoing[0].at[pl.ds(i * chunk_blocks + (1 - core) * core_len, core_len)]
        return param_copy(0, i, src, incoming[0].at[pl.ds(i * core_len, core_len)], core_peer)

    def chip_reduce(i):
        part = pl.ds(i * core_len, core_len)
        return param_copy(1, i, outgoing[1].at[part], incoming[1].at[part], chip_peer)

    def mid_reduce(i):
        part = pl.ds(i * mid_len, mid_len)
        return param_copy(2, i, outgoing[2].at[part], incoming[2].at[part], mid_peer)

    def mid_gather(i):
        part = wtd.at[pl.ds(i * chunk_blocks + mid_off, mid_len)]
        return param_copy(3, i, part, part, mid_peer)

    def chip_gather(i):
        part = wtd.at[pl.ds(i * chunk_blocks + core_off, core_len)]
        return param_copy(4, i, part, part, chip_peer)

    def core_gather(i):
        part = wtd.at[pl.ds(i * chunk_blocks + core_off, core_len)]
        return param_copy(5, i, part, part, core_peer)

    def adj_copy(i, d):
        part = pl.ds(i * chunk_freqs, chunk_freqs)
        return pltpu.make_async_remote_copy(
            src_ref=adj.at[part, freq_peer(d)],
            dst_ref=own_ref.at[freq_me, part],
            send_sem=adj_send.at[d - 1, i],
            recv_sem=adj_recv.at[d - 1, i],
            device_id={"freq": freq_peer(d)},
            device_id_type=MESH,
        )

    def own_adj_copy(i):
        part = pl.ds(i * chunk_freqs, chunk_freqs)
        return pltpu.make_async_copy(
            adj.at[part, freq_me], own_ref.at[freq_me, part], local_sem.at[i + 1]
        )

    own_spec_copy().start()

    @pl.loop(0, chunks)
    def _(i):
        green_copy(i).start()

    for f in range(freq_loc):
        for b in range(col_blocks):
            lanes = slice(b * LANES, (b + 1) * LANES)
            inv_blocks[f * col_blocks + b] = inv_ref[f : f + 1, lanes]
            for ri in range(2):
                lanes = slice(ri * sensors + b * LANES, ri * sensors + (b + 1) * LANES)
                obs_blocks[f * col_blocks + b, ri : ri + 1] = obs_ref[f : f + 1, lanes]

    pl.semaphore_wait(barrier, freq_count + 1 + (chip + side) % 2)

    @pl.loop(0, chunks)
    def _(i):
        for d in range(1, freq_count):
            spec_copy(i, d).start()

    own_spec_copy().wait()

    def combine(first, second, sign):
        pieces = []
        for j in range(freq_count):
            for ri in range(2):
                here = j * rows + ri * half_rows
                there = j * rows + (1 - ri) * half_rows
                a = first[here : here + half_rows]
                b = second[there : there + half_rows]
                pieces.append(a + b if (ri == 1) == (sign > 0) else a - b)
        return jnp.concatenate(pieces, axis=0)

    def forward(i):
        green_copy(i).wait()
        for d in range(1, freq_count):
            spec_copy(i, d).wait_recv()
        for g in range(chunk_freqs):
            f = i * chunk_freqs + g
            x = field[f].reshape(freq_count * rows, field.shape[3])
            first = jnp.dot(x, green[0, f], preferred_element_type=jnp.float32)
            second = jnp.dot(x, green[1, f], preferred_element_type=jnp.float32)
            data = combine(first, second, 1)
            for b in range(col_blocks):
                block = data[:, b * LANES : (b + 1) * LANES]
                acc[f * col_blocks + b] = block
                outgoing[0][f * col_blocks + b] = block.astype(jnp.bfloat16)
        core_reduce(i).start()

    def pass_inward(i):
        core_reduce(i).wait_recv()
        kept = pl.ds(i * chunk_blocks + core_off, core_len)
        part = pl.ds(i * core_len, core_len)
        total = acc[kept] + incoming[0][part].astype(jnp.float32)

        @pl.when(inner)
        def _():
            acc[kept] = total

        @pl.when(outer)
        def _():
            outgoing[1][part] = total.astype(jnp.bfloat16)
            chip_reduce(i).start()

    def cross(i):
        @pl.when(inner)
        def _():
            chip_reduce(i).wait_recv()
            kept = pl.ds(i * chunk_blocks + core_off, core_len)
            part = pl.ds(i * core_len, core_len)
            acc[kept] = acc[kept] + incoming[1][part].astype(jnp.float32)
            away = pl.ds(i * chunk_blocks + core_off + (1 - side) * mid_len, mid_len)
            outgoing[2][pl.ds(i * mid_len, mid_len)] = acc[away].astype(jnp.bfloat16)
            mid_reduce(i).start()

    def weigh(i):
        @pl.when(inner)
        def _():
            mid_reduce(i).wait_recv()
            for n in range(mid_len):
                b = i * chunk_blocks + mid_off + n
                total = acc[b] + incoming[2][i * mid_len + n].astype(jnp.float32)
                target = obs_blocks[b]
                weight = inv_blocks[b]
                pieces = []
                for j in range(freq_count):
                    for ri in range(2):
                        here = j * rows + ri * half_rows
                        pieces.append(
                            weight * (total[here : here + half_rows] - target[ri : ri + 1])
                        )
                wtd[b] = jnp.concatenate(pieces, axis=0).astype(jnp.bfloat16)
            mid_gather(i).start()

    def pass_outward(i):
        @pl.when(inner)
        def _():
            mid_gather(i).wait_recv()
            chip_gather(i).start()
            core_gather(i).start()

    def share(i):
        @pl.when(outer)
        def _():
            chip_gather(i).wait_recv()
            core_gather(i).start()

    def backward(i):
        core_gather(i).wait_recv()
        dims = (((1,), (1,)), ((), ()))
        for g in range(chunk_freqs):
            f = i * chunk_freqs + g
            w = jnp.concatenate([wtd[f * col_blocks + b] for b in range(col_blocks)], axis=1)
            first = lax.dot_general(w, green[0, f], dims, preferred_element_type=jnp.float32)
            second = lax.dot_general(w, green[1, f], dims, preferred_element_type=jnp.float32)
            back = combine(first, second, -1).astype(jnp.bfloat16)
            adj[f] = back.reshape(freq_count, rows, back.shape[1])
        for d in range(1, freq_count):
            adj_copy(i, d).start()
        own_adj_copy(i).start()

    stages = (forward, pass_inward, cross, weigh, pass_outward, share, backward)

    @pl.loop(0, chunks + stage_ticks[-1])
    def _(tick):
        for lag, stage in zip(stage_ticks, stages):
            @pl.when((tick >= lag) & (tick < chunks + lag))
            def _():
                stage(tick - lag)

    @pl.loop(0, chunks)
    def _(i):
        for d in range(1, freq_count):
            spec_copy(i, d).wait_send()
        core_reduce(i).wait_send()
        core_gather(i).wait_send()

        @pl.when(outer)
        def _():
            chip_reduce(i).wait_send()

        @pl.when(inner)
        def _():
            mid_reduce(i).wait_send()
            mid_gather(i).wait_send()
            chip_gather(i).wait_send()

        for d in range(1, freq_count):
            adj_copy(i, d).wait_send()
            adj_copy(i, d).wait_recv()
        own_adj_copy(i).wait()


def exchange(spec, green, observed, inv_noise, call_id):
    freq_count, freq_loc, rows, slab = spec.shape
    sensors = green.shape[3]
    col_blocks = sensors // LANES
    chunk_blocks = CHUNK_FREQS * col_blocks
    chunks = freq_loc // CHUNK_FREQS
    blocks = freq_loc * col_blocks
    all_rows = freq_count * rows
    bf16, f32 = jnp.bfloat16, jnp.float32
    dma = pltpu.SemaphoreType.DMA
    vmem = pl.BlockSpec(memory_space=pltpu.VMEM)
    flops = 16 * freq_loc * all_rows * slab * sensors
    return pl.pallas_call(
        functools.partial(exchange_kernel, freq_count, CHUNK_FREQS, STAGE_TICKS),
        out_shape=jax.ShapeDtypeStruct(spec.shape, bf16),
        in_specs=[vmem, pl.BlockSpec(memory_space=pltpu.HBM), vmem, vmem],
        out_specs=vmem,
        scratch_shapes=[
            pltpu.VMEM((blocks, 2, LANES), f32),
            pltpu.VMEM((blocks, 1, LANES), f32),
            pltpu.VMEM(green.shape, bf16),
            pltpu.VMEM((freq_loc, freq_count, rows, slab), bf16),
            pltpu.VMEM((blocks, all_rows, LANES), f32),
            [pltpu.VMEM((blocks // part, all_rows, LANES), bf16) for part in (1, 2, 4)],
            [pltpu.VMEM((blocks // part, all_rows, LANES), bf16) for part in (2, 2, 4)],
            pltpu.VMEM((blocks, all_rows, LANES), bf16),
            pltpu.VMEM((freq_loc, freq_count, rows, slab), bf16),
            dma((chunks,)),
            dma((freq_count - 1, chunks)),
            dma((freq_count - 1, chunks)),
            dma((6, chunks)),
            dma((6, chunks)),
            dma((freq_count - 1, chunks)),
            dma((freq_count - 1, chunks)),
            dma((chunks + 1,)),
        ],
        compiler_params=pltpu.CompilerParams(
            collective_id=call_id, has_side_effects=True, vmem_limit_bytes=20 * 2**20
        ),
        cost_estimate=pl.CostEstimate(
            flops=flops, bytes_accessed=2 * green.size, transcendentals=0
        ),
    )(spec, green, observed, inv_noise)


def fits_kernel(chain_shape, green_shape):
    chains_loc, slab = chain_shape[0], chain_shape[1]
    param_count = lax.axis_size("param")
    blocks = CHUNK_FREQS * (green_shape[3] // LANES)
    return (
        2 * chains_loc % 16 == 0
        and slab % LANES == 0
        and green_shape[3] % LANES == 0
        and green_shape[1] % CHUNK_FREQS == 0
        and param_count == 8
        and lax.axis_size("freq") > 1
        and blocks % 4 == 0
    )


def kernel_steps(chain_state, second_moment, noise, green, observed, inv_noise, temper):
    chains_loc, slab_rows, time_len = chain_state.shape
    freq_loc = green.shape[1]
    freq_count = lax.axis_size("freq")
    freq_total = freq_loc * freq_count
    table = spectral_table(time_len, freq_total)
    temper_cols = temper[:, None, None]
    current = chain_state
    moment = second_moment
    for step_num in range(noise.shape[0]):
        spec = jnp.einsum(
            "cpt,tj->jcp",
            current.astype(jnp.bfloat16),
            table,
            preferred_element_type=jnp.float32,
        ).astype(jnp.bfloat16)
        spec = spec.reshape(freq_count, freq_loc, 2 * chains_loc, slab_rows)
        own_adjoint = exchange(spec, green, observed, inv_noise, step_num)
        gradient = jnp.einsum(
            "jcp,tj->cpt",
            own_adjoint.reshape(2 * freq_total, chains_loc, slab_rows),
            table,
            preferred_element_type=jnp.float32,
        )
        drift_term = temper_cols * gradient + current
        moment = decay_rate * moment + (1.0 - decay_rate) * drift_term * drift_term
        precondition = lax.rsqrt(moment)
        current = (
            current
            - step_length * precondition * drift_term
            + math.sqrt(2.0 * step_length) * jnp.sqrt(precondition) * noise[step_num]
        )
    return (current, moment)


def on_device(chain_state, second_moment, noise, green, observed, inv_noise, temper):
    if fits_kernel(chain_state.shape, green.shape):
        return kernel_steps(
            chain_state, second_moment, noise, green, observed, inv_noise, temper
        )
    chains_loc, slab_rows, time_len = chain_state.shape
    freq_loc = green.shape[1]
    freq_count = lax.axis_size("freq")
    freq_total = freq_loc * freq_count
    chains = chains_loc * freq_count
    forward_table = spectral_table(time_len, freq_total)
    inverse_table = forward_table.T
    green_re = green[0]
    green_im = green[1]
    upper_rows = jnp.concatenate([green_re, green_im], axis=2)
    lower_rows = jnp.concatenate([-green_im, green_re], axis=2)
    kernel = jnp.concatenate([upper_rows, lower_rows], axis=1)
    weights = jnp.concatenate([inv_noise, inv_noise], axis=1)
    temper_cols = temper[:, None, None]
    current = chain_state
    moment = second_moment
    for step_num in range(noise.shape[0]):
        low_state = current.astype(jnp.bfloat16)
        local_spec = jnp.dot(
            low_state.reshape(chains_loc * slab_rows, time_len),
            forward_table,
            preferred_element_type=jnp.float32,
        )
        local_spec = local_spec.astype(jnp.bfloat16).reshape(chains_loc, slab_rows, 2 * freq_total)
        spectrum = lax.all_to_all(local_spec, "freq", split_axis=2, concat_axis=0, tiled=True)
        mixed_spec = (
            spectrum.reshape(chains, slab_rows, freq_loc, 2)
            .transpose(2, 0, 3, 1)
            .reshape(freq_loc, chains, 2 * slab_rows)
        )
        partial_data = jnp.einsum(
            "fcq,fqs->fcs", mixed_spec, kernel, preferred_element_type=jnp.float32
        )
        predicted = lax.psum(partial_data.astype(jnp.bfloat16), "param").astype(jnp.float32)
        weighted = (weights[:, None, :] * (predicted - observed[:, None, :])).astype(jnp.bfloat16)
        adjoint = jnp.einsum(
            "fcs,fqs->fcq", weighted, kernel, preferred_element_type=jnp.float32
        ).astype(jnp.bfloat16)
        adjoint = (
            adjoint.reshape(freq_loc, chains, 2, slab_rows)
            .transpose(1, 3, 0, 2)
            .reshape(chains, slab_rows, 2 * freq_loc)
        )
        own_adjoint = lax.all_to_all(adjoint, "freq", split_axis=0, concat_axis=2, tiled=True)
        gradient = jnp.dot(
            own_adjoint.reshape(chains_loc * slab_rows, 2 * freq_total),
            inverse_table,
            preferred_element_type=jnp.float32,
        )
        gradient = gradient.reshape(chains_loc, slab_rows, time_len)
        drift_term = temper_cols * gradient + current
        moment = decay_rate * moment + (1.0 - decay_rate) * drift_term * drift_term
        precondition = lax.rsqrt(moment)
        current = (
            current
            - step_length * precondition * drift_term
            + math.sqrt(2.0 * step_length) * jnp.sqrt(precondition) * noise[step_num]
        )
    return (current, moment)


def solution(mesh):
    return jax.shard_map(
        on_device,
        mesh=mesh,
        in_specs=(
            P("freq", "param", None),
            P("freq", "param", None),
            P(None, "freq", "param", None),
            P(None, "freq", "param", None),
            P("freq", None),
            P("freq", None),
            P("freq"),
        ),
        out_specs=(P("freq", "param", None), P("freq", "param", None)),
        check_vma=False,
    )
```

profile of v0, /device:TPU:0, one launch (start us, length us, event | category | flops | bytes accessed | tf_op | source)
XLA Modules:
  0.0 96.9 jit_solution(9474295912818922042)
XLA Ops:
  0.6 0.0 copy-start.2
  0.6 0.0 copy-start.1
  0.7 0.6 fusion.27
  1.3 0.1 copy.21
  1.4 0.1 reshape.141
  1.5 0.1 convert_element_type.47
  1.6 3.0 %fusion.8 = bf16[128,8,256]{2,0,1:T(8,128)(2,1)S(1)} fusion(bf16[512,128,1]{0,1,2:T(8,128)(2,1)S(1)} %reshape.141, f32[8,256,512]{2,1,0:T(8,128)} %param.7), kind=kOutput, calls=%fused_computation.14 | convolution fusion | flops 269746176 | bytes 4849664 | tf_op jit(solution)/shard_map/cpt,tj->jcp/dot_general | solution.py:366
  4.6 0.3 copy.22
  4.9 0.0 copy-done.2
  4.9 0.0 copy-done.1
  4.9 0.0 copy-start
  4.9 3.4 %copy-done = bf16[2,16,256,512]{3,2,1,0:T(8,128)(2,1)S(1)} copy-done((bf16[2,16,256,512]{3,2,1,0:T(8,128)(2,1)S(1)}, bf16[2,16,256,512]{3,2,1,0:T(8,128)(2,1)}, u32[]{:S(2)}) %copy-start) | copy-done | bytes 8388632
  8.3 0.0 copy-start.3
  8.3 0.0 copy-start.4
  8.3 0.0 copy-start.5
  8.3 40.0 %shard_map.86 = bf16[4,16,16,256]{3,2,1,0:T(8,128)(2,1)S(1)} custom-call(bf16[4,16,16,256]{3,2,1,0:T(8,128)(2,1)S(1)} %bitcast.32, bf16[2,16,256,512]{3,2,1,0:T(8,128)(2,1)S(1)} %copy-done, f32[16,1024]{1,0:T(8,128)S(1)} %copy-done.1, f32[16,512]{1,0:T(8,128)S(1)} %copy-done.2), custom_call_target="tpu_custom_call" | custom-call | flops 2147483648 | bytes 8388608 | tf_op jit(solution)/shard_map/pallas_call | solution.py:308
  48.3 0.0 slice-start
  48.3 0.0 copy-done.3
  48.3 0.0 copy-done.4
  48.3 0.0 copy-done.5
  48.4 0.0 slice-start.1
  48.4 4.8 %fusion.3 = (f32[8,256,512]{2,1,0:T(8,128)S(1)}, f32[8,256,512]{2,1,0:T(8,128)S(1)}) fusion(f32[2,8,256,512]{3,2,1,0:T(8,128)} %param.9, f32[8,256,512]{2,1,0:T(8,128)S(1)} %copy-done.3, f32[8,256,512]{2,1,0:T(8,128)S(1)} %copy-done.4, f32[8]{0:T(128)S(1)} %copy-done.5, bf16[512,128]{0,1:T(8,128)(2,1)S(1)} %convert_element_type.47, ...), kind=kOutput, calls=%fused_computation.7 | convolution fusion | flops 279969792 | bytes 21626912 | tf_op jit(solution)/shard_map/jcp,tj->cpt/dot_general | solution.py:374
  53.2 0.8 fusion.11
  54.0 0.3 copy.25
  54.3 0.0 slice-done
  54.3 0.0 slice-done.1
  54.3 35.3 %shard_map.87 = bf16[4,16,16,256]{3,2,1,0:T(8,128)(2,1)S(1)} custom-call(bf16[4,16,16,256]{3,2,1,0:T(8,128)(2,1)S(1)} %bitcast.33, bf16[2,16,256,512]{3,2,1,0:T(8,128)(2,1)S(1)} %bitcast.29, f32[16,1024]{1,0:T(8,128)S(1)} %copy-done.1, f32[16,512]{1,0:T(8,128)S(1)} %copy-done.2), custom_call_target="tpu_custom_call" | custom-call | flops 2147483648 | bytes 8388608 | tf_op jit(solution)/shard_map/pallas_call | solution.py:308
  89.6 7.3 %fusion.2 = (f32[8,256,512]{2,1,0:T(8,128)}, f32[8,256,512]{2,1,0:T(8,128)}) fusion(f32[2,8,256,512]{3,2,1,0:T(8,128)} %param.9, f32[8,256,512]{2,1,0:T(8,128)S(1)} %get-tuple-element.6, f32[8]{0:T(128)S(1)} %copy-done.5, f32[8,256,512]{2,1,0:T(8,128)S(1)} %copy-done.3, f32[8,256,512]{2,1,0:T(8,128)S(1)} %get-tuple-element.7, ...), kind=kOutput, calls=%fused_computation.5 | convolution fusion | flops 286261248 | bytes 30015520 | tf_op jit(solution)/shard_map/jcp,tj->cpt/dot_general | solution.py:374
  (3 shorter events, 0.0 us)
Async XLA Ops:
  0.6 4.3 %copy-start.2 = (f32[16,512]{1,0:T(8,128)S(1)}, f32[16,512]{1,0:T(8,128)}, u32[]{:S(2)}) copy-start(f32[16,512]{1,0:T(8,128)} %inv_ref.3) | copy-start | bytes 98308
  0.6 4.3 %copy-start.1 = (f32[16,1024]{1,0:T(8,128)S(1)}, f32[16,1024]{1,0:T(8,128)}, u32[]{:S(2)}) copy-start(f32[16,1024]{1,0:T(8,128)} %obs_ref.3) | copy-start | bytes 196612
  4.9 3.4 %copy-start = (bf16[2,16,256,512]{3,2,1,0:T(8,128)(2,1)S(1)}, bf16[2,16,256,512]{3,2,1,0:T(8,128)(2,1)}, u32[]{:S(2)}) copy-start(bf16[2,16,256,512]{3,2,1,0:T(8,128)(2,1)} %green_hbm.3) | copy-start | bytes 25165828
  8.3 40.0 %copy-start.3 = (f32[8,256,512]{2,1,0:T(8,128)S(1)}, f32[8,256,512]{2,1,0:T(8,128)}, u32[]{:S(2)}) copy-start(f32[8,256,512]{2,1,0:T(8,128)} %param.7) | copy-start | bytes 12582916
  8.3 40.0 %copy-start.4 = (f32[8,256,512]{2,1,0:T(8,128)S(1)}, f32[8,256,512]{2,1,0:T(8,128)}, u32[]{:S(2)}) copy-start(f32[8,256,512]{2,1,0:T(8,128)} %param.8) | copy-start | bytes 12582916
  8.3 40.1 %copy-start.5 = (f32[8]{0:T(128)S(1)}, f32[8]{0:T(128)}, u32[]{:S(2)}) copy-start(f32[8]{0:T(128)} %param.13) | copy-start | bytes 100
  48.3 6.0 %slice-start = ((s8[8388608]{0:T(1024)(128)(4,1)}), s8[4194304]{0:T(1024)(128)(4,1)S(1)}, s32[]{:S(2)}) async-start(s8[8388608]{0:T(1024)(128)(4,1)} %bitcast.28), calls=%async_computation | async-start | bytes 8388608
  48.4 5.9 %slice-start.1 = ((s8[8388608]{0:T(1024)(128)(4,1)}), s8[4194304]{0:T(1024)(128)(4,1)S(1)}, s32[]{:S(2)}) async-start(s8[8388608]{0:T(1024)(128)(4,1)} %bitcast.28), calls=%async_computation.1 | async-start | bytes 8388608
where the time goes:
time: 97.1 us; the launch traced here: 96.9 us
  Pallas kernels  75.3 us (78%)
  matrix products  16 us (16%)
  local copies, waits for them, and re-layouts  4.25 us (4%)
    pallas_call x2, Pallas kernels, exchange(): pl.pallas_call(functools.partial(exchange_kernel, freq_count, CHUNK_FREQS...  75.3 us
    dot_general x2, matrix products, kernel_steps(): jnp.einsum('jcp,tj->cpt', own_adjoint.reshape(2 * freq_total, chains_loc,...  12.1 us
    dot_general x2, matrix products, kernel_steps(): jnp.einsum('cpt,tj->jcp', current.astype(jnp.bfloat16), table, preferred_...  3.84 us
    unnamed x16, local copies, waits for them, and re-layouts  3.41 us

commit v1 on v0

v1 whole, which is shorter than its diff:
```python
import functools
import math

import jax
import jax.numpy as jnp
from jax import lax
from jax.experimental import pallas as pl
from jax.experimental.pallas import tpu as pltpu
from jax.sharding import PartitionSpec as P

decay_rate = 0.9
step_length = 0.5
MESH = pl.DeviceIdType.MESH
LANES = 128
CHUNK_FREQS = 1
CORE_LAG = 2
HOP_LAG = 3
GATHER_LAG = 2


def spectral_table(time_len, freq_total):
    time_index = jnp.arange(time_len, dtype=jnp.int32)[:, None]
    wave_number = jnp.arange(freq_total, dtype=jnp.int32)[None, :] + 1
    phase_angle = (time_index * wave_number % time_len).astype(jnp.float32) * (
        2.0 * math.pi / time_len
    )
    columns_table = jnp.stack([jnp.cos(phase_angle), -jnp.sin(phase_angle)], axis=-1).reshape(
        time_len, 2 * freq_total
    )
    return (columns_table / math.sqrt(time_len)).astype(jnp.bfloat16)


def steps_kernel(
    freq_count, param_count, chunk_freqs,
    table_ref, temper_ref, obs_ref, inv_ref, state_hbm, moment_hbm, noise_hbm, green_hbm,
    adj_all, state, moment, last_noise,
    obs_rows, inv_rows, green, noise, rows32, spec, field, acc, core_out, core_in,
    up_out, up_in, down_out, down_in, wtd, adj,
    state_sem, green_sem, moment_sem, noise_sem, spec_send, spec_recv,
    line_send, line_recv, adj_send, adj_recv,
):
    freq_me = lax.axis_index("freq")
    param_me = lax.axis_index("param")
    steps, freq_loc = field.shape[0], field.shape[1]
    rows, slab = field.shape[3], field.shape[4]
    chains_loc = rows // 2
    all_rows, half = acc.shape[1], acc.shape[2]
    sensors = 2 * half
    col_blocks = slab // LANES
    columns = table_ref.shape[0]
    chunks = freq_loc // chunk_freqs
    line = param_count // 2
    core = lax.rem(param_me, 2)
    chip = param_me // 2
    core_peer = param_me + 1 - 2 * core
    above, below = param_me + 2, param_me - 2
    has_above, has_below = chip < line - 1, chip > 0

    def freq_peer(d):
        return lax.rem(freq_me + d, freq_count)

    barrier = pltpu.get_barrier_semaphore()
    for d in range(1, freq_count):
        pl.semaphore_signal(barrier, inc=1, device_id={"freq": freq_peer(d)}, device_id_type=MESH)
    pl.semaphore_signal(barrier, inc=1, device_id={"param": core_peer}, device_id_type=MESH)

    @pl.when(has_above)
    def _():
        pl.semaphore_signal(barrier, inc=1, device_id={"param": above}, device_id_type=MESH)

    @pl.when(has_below)
    def _():
        pl.semaphore_signal(barrier, inc=1, device_id={"param": below}, device_id_type=MESH)

    def state_copy(c):
        return pltpu.make_async_copy(state_hbm.at[c], state.at[c], state_sem.at[c])

    def green_copy(f):
        return pltpu.make_async_copy(green_hbm.at[:, f], green.at[f], green_sem.at[f])

    def moment_copy():
        return pltpu.make_async_copy(moment_hbm, moment, moment_sem.at[0])

    def noise_copy(s):
        return pltpu.make_async_copy(noise_hbm.at[s], noise.at[s], noise_sem.at[s])

    def last_noise_copy():
        return pltpu.make_async_copy(noise_hbm.at[steps - 1], last_noise, noise_sem.at[steps - 1])

    def spec_copy(s, i, d):
        part = pl.ds(i * chunk_freqs, chunk_freqs)
        return pltpu.make_async_remote_copy(
            src_ref=spec.at[s, freq_peer(d), part],
            dst_ref=field.at[s, part, freq_me],
            send_sem=spec_send.at[s, d - 1, i],
            recv_sem=spec_recv.at[s, d - 1, i],
            device_id={"freq": freq_peer(d)},
            device_id_type=MESH,
        )

    def param_copy(k, s, i, src, dst, peer):
        part = pl.ds(i * chunk_freqs, chunk_freqs)
        return pltpu.make_async_remote_copy(
            src_ref=src.at[part],
            dst_ref=dst.at[part],
            send_sem=line_send.at[k, s, i],
            recv_sem=line_recv.at[k, s, i],
            device_id={"param": peer},
            device_id_type=MESH,
        )

    def core_reduce(s, i):
        return param_copy(0, s, i, core_out.at[s], core_in.at[s], core_peer)

    def core_gather(s, i):
        return param_copy(1, s, i, wtd.at[s, core], wtd.at[s, core], core_peer)

    def up_copy(s, i):
        return param_copy(2, s, i, up_out.at[s], up_in.at[s], above)

    def down_copy(s, i):
        return param_copy(3, s, i, down_out.at[s], down_in.at[s], below)

    def adj_copy(s, i, d):
        part = pl.ds(i * chunk_freqs, chunk_freqs)
        return pltpu.make_async_remote_copy(
            src_ref=adj.at[s, part, freq_peer(d)],
            dst_ref=adj_all.at[s, freq_me, part],
            send_sem=adj_send.at[s, d - 1, i],
            recv_sem=adj_recv.at[s, d - 1, i],
            device_id={"freq": freq_peer(d)},
            device_id_type=MESH,
        )

    def transform(c, low):
        dims = (((1,), (1,)), ((), ()))
        result = lax.dot_general(table_ref[...], low, dims, preferred_element_type=jnp.float32)
        for b in range(col_blocks):
            block = result[:, b * LANES : (b + 1) * LANES]
            rows32[b, pl.ds(c, columns, stride=chains_loc)] = block

    def send_spectrum(s):
        @pl.loop(0, chunks)
        def _(i):
            for g in range(chunk_freqs):
                f = i * chunk_freqs + g
                for d in range(freq_count):
                    first = pl.multiple_of((freq_peer(d) * freq_loc + f) * rows, rows)
                    pieces = [rows32[b, pl.ds(first, rows)] for b in range(col_blocks)]
                    tile = jnp.concatenate(pieces, axis=1).astype(jnp.bfloat16)
                    if d == 0:
                        field[s, f, freq_me] = tile
                    else:
                        spec[s, freq_peer(d), f] = tile
            for d in range(1, freq_count):
                spec_copy(s, i, d).start()

    @pl.loop(0, chains_loc)
    def _(c):
        state_copy(c).start()

    for f in range(freq_loc):
        first = pl.multiple_of(core * half, half)
        inv_rows[f] = inv_ref[f : f + 1, pl.ds(first, half)]
        for ri in range(2):
            first = pl.multiple_of(ri * sensors + core * half, half)
            obs_rows[f, ri : ri + 1] = obs_ref[f : f + 1, pl.ds(first, half)]

    @pl.loop(0, chains_loc)
    def _(c):
        state_copy(c).wait()
        transform(c, state[c].astype(jnp.bfloat16))

    @pl.loop(0, freq_loc)
    def _(f):
        green_copy(f).start()

    moment_copy().start()
    for s in range(steps - 1):
        noise_copy(s).start()
    last_noise_copy().start()

    met = has_above.astype(jnp.int32) + has_below.astype(jnp.int32)
    pl.semaphore_wait(barrier, freq_count + met)
    send_spectrum(0)

    def turned(x, sign):
        wide = x.astype(jnp.float32)
        pieces = []
        for j in range(freq_count):
            re = wide[j * rows : j * rows + chains_loc]
            im = wide[j * rows + chains_loc : (j + 1) * rows]
            pieces += [im, -re] if sign < 0 else [-im, re]
        return jnp.concatenate(pieces, axis=0).astype(jnp.bfloat16)

    def forward(s, i):
        @pl.when(s == 0)
        def _():
            for g in range(chunk_freqs):
                green_copy(i * chunk_freqs + g).wait()

        for d in range(1, freq_count):
            spec_copy(s, i, d).wait_recv()
        for g in range(chunk_freqs):
            f = i * chunk_freqs + g
            x = field[s, f].reshape(all_rows, slab)
            both = jnp.concatenate([x, turned(x, 1)], axis=1)
            weights = green[f].reshape(2 * slab, sensors)
            data = jnp.dot(both, weights, preferred_element_type=jnp.float32)
            low, high = data[:, :half], data[:, half:]
            acc[f] = jnp.where(core == 0, low, high)
            core_out[s, f] = jnp.where(core == 0, high, low).astype(jnp.bfloat16)
        core_reduce(s, i).start()

    def merge(s, i):
        core_reduce(s, i).wait_recv()
        part = pl.ds(i * chunk_freqs, chunk_freqs)
        total = acc[part] + core_in[s, part].astype(jnp.float32)
        acc[part] = total

        @pl.when(chip == 0)
        def _():
            up_out[s, part] = total.astype(jnp.bfloat16)
            up_copy(s, i).start()

        @pl.when(chip == line - 1)
        def _():
            down_out[s, part] = total.astype(jnp.bfloat16)
            down_copy(s, i).start()

    def pass_up(s, i):
        up_copy(s, i).wait_recv()
        part = pl.ds(i * chunk_freqs, chunk_freqs)
        total = acc[part] + up_in[s, part].astype(jnp.float32)
        up_out[s, part] = total.astype(jnp.bfloat16)
        up_copy(s, i).start()

    def pass_down(s, i):
        down_copy(s, i).wait_recv()
        part = pl.ds(i * chunk_freqs, chunk_freqs)
        total = acc[part] + down_in[s, part].astype(jnp.float32)
        down_out[s, part] = total.astype(jnp.bfloat16)
        down_copy(s, i).start()

    def weigh(s, i):
        part = pl.ds(i * chunk_freqs, chunk_freqs)

        @pl.when(chip == line - 1)
        def _():
            up_copy(s, i).wait_recv()

        @pl.when(chip == 0)
        def _():
            down_copy(s, i).wait_recv()

        @pl.when(has_below)
        def _():
            acc[part] = acc[part] + up_in[s, part].astype(jnp.float32)

        @pl.when(has_above)
        def _():
            acc[part] = acc[part] + down_in[s, part].astype(jnp.float32)

        for g in range(chunk_freqs):
            f = i * chunk_freqs + g
            total = acc[f]
            target = obs_rows[f]
            weight = inv_rows[f]
            pieces = []
            for j in range(freq_count):
                for ri in range(2):
                    here = j * rows + ri * chains_loc
                    apart = total[here : here + chains_loc] - target[ri : ri + 1]
                    pieces.append(weight * apart)
            wtd[s, core, f] = jnp.concatenate(pieces, axis=0).astype(jnp.bfloat16)
        core_gather(s, i).start()

    def backward(s, i):
        core_gather(s, i).wait_recv()
        dims = (((1,), (1,)), ((), ()))
        for g in range(chunk_freqs):
            f = i * chunk_freqs + g
            w = jnp.concatenate([wtd[s, 0, f], wtd[s, 1, f]], axis=1)
            first = lax.dot_general(w, green[f, 0], dims, preferred_element_type=jnp.float32)
            second = lax.dot_general(
                turned(w, -1), green[f, 1], dims, preferred_element_type=jnp.float32
            )
            back = (first + second).astype(jnp.bfloat16)
            adj[s, f] = back.reshape(freq_count, rows, slab)
            adj_all[s, freq_me, f] = adj[s, f, freq_me]
        for d in range(1, freq_count):
            adj_copy(s, i, d).start()

    up_depth, down_depth = chip, line - 1 - chip
    deepest = jnp.maximum(up_depth, down_depth)
    up_lag = CORE_LAG + HOP_LAG * up_depth
    down_lag = CORE_LAG + HOP_LAG * down_depth
    weigh_lag = CORE_LAG + HOP_LAG * deepest
    inside = has_above & has_below

    @pl.loop(0, steps)
    def _(s):
        @pl.loop(0, chunks + CORE_LAG + HOP_LAG * (line - 1) + GATHER_LAG)
        def _(tick):
            def stage(lag, work, allowed=None):
                due = (tick >= lag) & (tick < chunks + lag)

                @pl.when(due if allowed is None else due & allowed)
                def _():
                    work(s, tick - lag)

            stage(CORE_LAG, merge)
            stage(up_lag, pass_up, inside)
            stage(down_lag, pass_down, inside)
            stage(weigh_lag, weigh)
            stage(0, forward)
            stage(weigh_lag + GATHER_LAG, backward)

        @pl.loop(0, chunks)
        def _(i):
            for d in range(1, freq_count):
                adj_copy(s, i, d).wait_recv()

        @pl.when(s < steps - 1)
        def _():
            @pl.when(s == 0)
            def _():
                moment_copy().wait()

            noise_copy(s).wait()

            @pl.loop(0, freq_count)
            def _(j):
                for f in range(freq_loc):
                    first = pl.multiple_of((j * freq_loc + f) * rows, rows)
                    tile = adj_all[s, j, f].astype(jnp.float32)
                    for b in range(col_blocks):
                        block = tile[:, b * LANES : (b + 1) * LANES]
                        rows32[b, pl.ds(first, rows)] = block

            @pl.loop(0, chains_loc)
            def _(c):
                current, spread = advance(
                    c, rows32, table_ref, temper_ref, state[c], moment[c], noise[s, c]
                )
                state[c] = current
                moment[c] = spread
                transform(c, current.astype(jnp.bfloat16))

            send_spectrum(s + 1)

    last_noise_copy().wait()

    @pl.loop(0, steps)
    def _(s):
        @pl.loop(0, chunks)
        def _(i):
            for d in range(1, freq_count):
                spec_copy(s, i, d).wait_send()
                adj_copy(s, i, d).wait_send()
            core_reduce(s, i).wait_send()
            core_gather(s, i).wait_send()

            @pl.when(has_above)
            def _():
                up_copy(s, i).wait_send()

            @pl.when(has_below)
            def _():
                down_copy(s, i).wait_send()


def advance(c, rows32, table_ref, temper_ref, current, spread, push):
    columns, chains_loc = table_ref.shape[0], rows32.shape[1] // table_ref.shape[0]
    pieces = [
        rows32[b, pl.ds(c, columns, stride=chains_loc)] for b in range(rows32.shape[0])
    ]
    mine = jnp.concatenate(pieces, axis=1).astype(jnp.bfloat16)
    gradient = lax.dot_general(
        mine, table_ref[...], (((0,), (0,)), ((), ())), preferred_element_type=jnp.float32
    )
    drift_term = temper_ref[c] * gradient + current
    spread = decay_rate * spread + (1.0 - decay_rate) * drift_term * drift_term
    precondition = lax.rsqrt(spread)
    root = precondition * lax.rsqrt(precondition)
    current = (
        current
        - step_length * precondition * drift_term
        + math.sqrt(2.0 * step_length) * root * push
    )
    return current, spread


def final_kernel(
    table_ref, temper_ref, adj_all, state, moment, push, state_hbm, moment_hbm,
    rows32, new_state, new_moment, state_sem, moment_sem,
):
    last = adj_all.shape[0] - 1
    freq_count, freq_loc, rows, slab = adj_all.shape[1:]

    def state_copy(c):
        return pltpu.make_async_copy(new_state.at[c], state_hbm.at[c], state_sem.at[c])

    def moment_copy(c):
        return pltpu.make_async_copy(new_moment.at[c], moment_hbm.at[c], moment_sem.at[c])

    @pl.loop(0, freq_count)
    def _(j):
        for f in range(freq_loc):
            first = pl.multiple_of((j * freq_loc + f) * rows, rows)
            tile = adj_all[last, j, f].astype(jnp.float32)
            for b in range(slab // LANES):
                rows32[b, pl.ds(first, rows)] = tile[:, b * LANES : (b + 1) * LANES]

    @pl.loop(0, state.shape[0])
    def _(c):
        current, spread = advance(
            c, rows32, table_ref, temper_ref, state[c], moment[c], push[c]
        )
        new_state[c] = current
        new_moment[c] = spread
        state_copy(c).start()
        moment_copy(c).start()

    @pl.loop(0, state.shape[0])
    def _(c):
        state_copy(c).wait()
        moment_copy(c).wait()


def fits_kernel(chain_shape, green_shape):
    chains_loc, slab = chain_shape[0], chain_shape[1]
    param_count = lax.axis_size("param")
    return (
        chains_loc % 8 == 0
        and slab % LANES == 0
        and chain_shape[2] % LANES == 0
        and green_shape[3] % (2 * LANES) == 0
        and green_shape[1] % CHUNK_FREQS == 0
        and param_count == 8
        and lax.axis_size("freq") > 1
    )


def kernel_steps(chain_state, second_moment, noise, green, observed, inv_noise, temper):
    chains_loc, slab, time_len = chain_state.shape
    freq_loc, sensors = green.shape[1], green.shape[3]
    steps = noise.shape[0]
    freq_count, param_count = lax.axis_size("freq"), lax.axis_size("param")
    columns = 2 * freq_loc * freq_count
    table = spectral_table(time_len, freq_loc * freq_count).T
    chunks = freq_loc // CHUNK_FREQS
    rows, half = 2 * chains_loc, sensors // 2
    all_rows = freq_count * rows
    bf16, f32 = jnp.bfloat16, jnp.float32
    dma = pltpu.SemaphoreType.DMA
    vmem = pl.BlockSpec(memory_space=pltpu.VMEM)
    smem = pl.BlockSpec(memory_space=pltpu.SMEM)
    hbm = pl.BlockSpec(memory_space=pltpu.HBM)
    line_buf = pltpu.VMEM((steps, freq_loc, all_rows, half), bf16)
    rows32 = pltpu.VMEM((slab // LANES, columns * chains_loc, LANES), f32)
    peers = freq_count - 1
    adj_all, state, moment, push = pl.pallas_call(
        functools.partial(steps_kernel, freq_count, param_count, CHUNK_FREQS),
        out_shape=[
            jax.ShapeDtypeStruct((steps, freq_count, freq_loc, rows, slab), bf16),
            jax.ShapeDtypeStruct(chain_state.shape, f32),
            jax.ShapeDtypeStruct(chain_state.shape, f32),
            jax.ShapeDtypeStruct(chain_state.shape, f32),
        ],
        in_specs=[vmem, smem, vmem, vmem, hbm, hbm, hbm, hbm],
        out_specs=[vmem, vmem, vmem, vmem],
        scratch_shapes=[
            pltpu.VMEM((freq_loc, 2, half), f32),
            pltpu.VMEM((freq_loc, 1, half), f32),
            pltpu.VMEM((freq_loc, 2, slab, sensors), bf16),
            pltpu.VMEM((max(steps - 1, 1),) + chain_state.shape, f32),
            rows32,
            pltpu.VMEM((steps, freq_count, freq_loc, rows, slab), bf16),
            pltpu.VMEM((steps, freq_loc, freq_count, rows, slab), bf16),
            pltpu.VMEM((freq_loc, all_rows, half), f32),
            line_buf, line_buf, line_buf, line_buf, line_buf, line_buf,
            pltpu.VMEM((steps, 2, freq_loc, all_rows, half), bf16),
            pltpu.VMEM((steps, freq_loc, freq_count, rows, slab), bf16),
            dma((chains_loc,)),
            dma((freq_loc,)),
            dma((1,)),
            dma((steps,)),
            dma((steps, peers, chunks)),
            dma((steps, peers, chunks)),
            dma((4, steps, chunks)),
            dma((4, steps, chunks)),
            dma((steps, peers, chunks)),
            dma((steps, peers, chunks)),
        ],
        compiler_params=pltpu.CompilerParams(
            collective_id=0, has_side_effects=True, vmem_limit_bytes=44 * 2**20
        ),
    )(table, temper, observed, inv_noise, chain_state, second_moment, noise, green)
    return pl.pallas_call(
        final_kernel,
        out_shape=[
            jax.ShapeDtypeStruct(chain_state.shape, f32),
            jax.ShapeDtypeStruct(chain_state.shape, f32),
        ],
        in_specs=[vmem, smem, vmem, vmem, vmem, vmem],
        out_specs=[hbm, hbm],
        scratch_shapes=[
            rows32,
            pltpu.VMEM(chain_state.shape, f32),
            pltpu.VMEM(chain_state.shape, f32),
            dma((chains_loc,)),
            dma((chains_loc,)),
        ],
        compiler_params=pltpu.CompilerParams(vmem_limit_bytes=14 * 2**20),
    )(table, temper, adj_all, state, moment, push)


def on_device(chain_state, second_moment, noise, green, observed, inv_noise, temper):
    if fits_kernel(chain_state.shape, green.shape):
        return kernel_steps(
            chain_state, second_moment, noise, green, observed, inv_noise, temper
        )
    chains_loc, slab_rows, time_len = chain_state.shape
    freq_loc = green.shape[1]
    freq_count = lax.axis_size("freq")
    freq_total = freq_loc * freq_count
    chains = chains_loc * freq_count
    forward_table = spectral_table(time_len, freq_total)
    inverse_table = forward_table.T
    green_re = green[0]
    green_im = green[1]
    upper_rows = jnp.concatenate([green_re, green_im], axis=2)
    lower_rows = jnp.concatenate([-green_im, green_re], axis=2)
    kernel = jnp.concatenate([upper_rows, lower_rows], axis=1)
    weights = jnp.concatenate([inv_noise, inv_noise], axis=1)
    temper_cols = temper[:, None, None]
    current = chain_state
    moment = second_moment
    for step_num in range(noise.shape[0]):
        low_state = current.astype(jnp.bfloat16)
        local_spec = jnp.dot(
            low_state.reshape(chains_loc * slab_rows, time_len),
            forward_table,
            preferred_element_type=jnp.float32,
        )
        local_spec = local_spec.astype(jnp.bfloat16).reshape(chains_loc, slab_rows, 2 * freq_total)
        spectrum = lax.all_to_all(local_spec, "freq", split_axis=2, concat_axis=0, tiled=True)
        mixed_spec = (
            spectrum.reshape(chains, slab_rows, freq_loc, 2)
            .transpose(2, 0, 3, 1)
            .reshape(freq_loc, chains, 2 * slab_rows)
        )
        partial_data = jnp.einsum(
            "fcq,fqs->fcs", mixed_spec, kernel, preferred_element_type=jnp.float32
        )
        predicted = lax.psum(partial_data.astype(jnp.bfloat16), "param").astype(jnp.float32)
        weighted = (weights[:, None, :] * (predicted - observed[:, None, :])).astype(jnp.bfloat16)
        adjoint = jnp.einsum(
            "fcs,fqs->fcq", weighted, kernel, preferred_element_type=jnp.float32
        ).astype(jnp.bfloat16)
        adjoint = (
            adjoint.reshape(freq_loc, chains, 2, slab_rows)
            .transpose(1, 3, 0, 2)
            .reshape(chains, slab_rows, 2 * freq_loc)
        )
        own_adjoint = lax.all_to_all(adjoint, "freq", split_axis=0, concat_axis=2, tiled=True)
        gradient = jnp.dot(
            own_adjoint.reshape(chains_loc * slab_rows, 2 * freq_total),
            inverse_table,
            preferred_element_type=jnp.float32,
        )
        gradient = gradient.reshape(chains_loc, slab_rows, time_len)
        drift_term = temper_cols * gradient + current
        moment = decay_rate * moment + (1.0 - decay_rate) * drift_term * drift_term
        precondition = lax.rsqrt(moment)
        current = (
            current
            - step_length * precondition * drift_term
            + math.sqrt(2.0 * step_length) * jnp.sqrt(precondition) * noise[step_num]
        )
    return (current, moment)


def solution(mesh):
    return jax.shard_map(
        on_device,
        mesh=mesh,
        in_specs=(
            P("freq", "param", None),
            P("freq", "param", None),
            P(None, "freq", "param", None),
            P(None, "freq", "param", None),
            P("freq", None),
            P("freq", None),
            P("freq"),
        ),
        out_specs=(P("freq", "param", None), P("freq", "param", None)),
        check_vma=False,
    )
```

time: 97.1 us -> 95.1 us (0.979)
  matrix products: 16 us -> 0 us
  Pallas kernels: 75.3 us -> 88.9 us
    dot_general x4 -> x0, matrix products: 16 us -> none  [the longest x2 12.1 us: kernel_steps(): jnp.einsum('jcp,tj->cpt', own_adjoint.reshape(2 * freq_total, chains_loc,...]
    pallas_call x2, Pallas kernels: 75.3 us -> 88.9 us  [the longest x1 83.5 us: kernel_steps(): pl.pallas_call(functools.partial(steps_kernel, freq_count, param_count, C...]
    unnamed x16 -> x8, local copies, waits for them, and re-layouts: 3.41 us -> 4.43 us
where the time goes in v1:
time: 95.1 us; the launch traced here: 94.8 us
  Pallas kernels  88.9 us (93%)
  local copies, waits for them, and re-layouts  4.62 us (5%)
    pallas_call x1, Pallas kernels, kernel_steps(): pl.pallas_call(functools.partial(steps_kernel, freq_count, param_count, C...  83.5 us
    pallas_call x1, Pallas kernels, kernel_steps(): pl.pallas_call(final_kernel, out_shape=[jax.ShapeDtypeStruct(chain_state....  5.31 us
    unnamed x8, local copies, waits for them, and re-layouts  4.43 us

profile of v1, /device:TPU:0, one launch (start us, length us, event | category | flops | bytes accessed | tf_op | source)
XLA Modules:
  0.0 94.8 jit_solution(14498234902369001886)
XLA Ops:
  0.6 0.6 fusion.7
  1.3 0.1 copy.9
  1.4 0.1 convert_element_type.24
  1.5 0.0 copy-start.1
  1.5 0.8 copy-done.1
  2.3 0.0 copy-start.2
  2.3 0.8 copy-done.2
  3.1 0.0 copy-start.3
  3.1 0.7 copy-done.3
  3.7 83.5 %shard_map.86 = (bf16[2,4,16,16,256]{4,3,2,1,0:T(8,128)(2,1)S(1)}, f32[8,256,512]{2,1,0:T(8,128)S(1)}, f32[8,256,512]{2,1,0:T(8,128)S(1)}, f32[8,256,512]{2,1,0:T(8,128)}) custom-call(bf16[128,512]{1,0:T(8,128)(2,1)S(1)} %bitcast.3, f32[8]{0:T(128)S(1)} %copy-done.3, f32[16,1024]{1,0:T(8,128)S(1)} %copy-done.1, f32[16,512]{1,0:T(8,128)S(1)} %copy-done.2, ...), custom_call_target="tpu_custom_call" | custom-call | tf_op jit(solution)/shard_map/pallas_call | solution.py:463
  87.3 0.0 copy-start
  87.3 2.2 %copy-done = f32[8,256,512]{2,1,0:T(8,128)S(1)} copy-done((f32[8,256,512]{2,1,0:T(8,128)S(1)}, f32[8,256,512]{2,1,0:T(8,128)}, u32[]{:S(2)}) %copy-start) | copy-done | bytes 4194328
  89.5 5.3 %shard_map.87 = (f32[8,256,512]{2,1,0:T(8,128)}, f32[8,256,512]{2,1,0:T(8,128)}) custom-call(bf16[128,512]{1,0:T(8,128)(2,1)S(1)} %bitcast.4, f32[8]{0:T(128)S(1)} %copy-done.3, bf16[2,4,16,16,256]{4,3,2,1,0:T(8,128)(2,1)S(1)} %get-tuple-element.6.adj_all, f32[8,256,512]{2,1,0:T(8,128)S(1)} %get-tuple-element.7.state, ...), custom_call_target="tpu_custom_call" | custom-call | tf_op jit(solution)/shard_map/pallas_call | solution.py:500
  (2 shorter events, 0.0 us)
Async XLA Ops:
  1.5 0.8 copy-start.1
  2.3 0.8 copy-start.2
  3.1 0.7 copy-start.3
  87.3 2.2 %copy-start = (f32[8,256,512]{2,1,0:T(8,128)S(1)}, f32[8,256,512]{2,1,0:T(8,128)}, u32[]{:S(2)}) copy-start(f32[8,256,512]{2,1,0:T(8,128)} %get-tuple-element.9.push) | copy-start | bytes 12582916

commit v2 on v1

--- a/solution.py
+++ b/solution.py
@@ -13,9 +13,9 @@
 MESH = pl.DeviceIdType.MESH
 LANES = 128
 CHUNK_FREQS = 1
-CORE_LAG = 2
-HOP_LAG = 3
-GATHER_LAG = 2
+CORE_LAG = 3
+HOP_LAG = 5
+GATHER_LAG = 4
 
 
 def spectral_table(time_len, freq_total):
@@ -32,11 +32,11 @@
 
 def steps_kernel(
     freq_count, param_count, chunk_freqs,
-    table_ref, temper_ref, obs_ref, inv_ref, state_hbm, moment_hbm, noise_hbm, green_hbm,
-    adj_all, state, moment, last_noise,
-    obs_rows, inv_rows, green, noise, rows32, spec, field, acc, core_out, core_in,
+    table_ref, temper_hbm, obs_hbm, inv_hbm, state_hbm, moment_hbm, noise_hbm, green_hbm,
+    adj_all, state, moment,
+    temper_ref, obs_all, inv_all, obs_rows, inv_rows, green, noise, rows32, spec, field, acc, core_out, core_in,
     up_out, up_in, down_out, down_in, wtd, adj,
-    state_sem, green_sem, moment_sem, noise_sem, spec_send, spec_recv,
+    small_sem, state_sem, green_sem, moment_sem, noise_sem, spec_send, spec_recv,
     line_send, line_recv, adj_send, adj_recv,
 ):
     freq_me = lax.axis_index("freq")
@@ -78,22 +78,28 @@
     def green_copy(f):
         return pltpu.make_async_copy(green_hbm.at[:, f], green.at[f], green_sem.at[f])
 
-    def moment_copy():
-        return pltpu.make_async_copy(moment_hbm, moment, moment_sem.at[0])
-
-    def noise_copy(s):
-        return pltpu.make_async_copy(noise_hbm.at[s], noise.at[s], noise_sem.at[s])
-
-    def last_noise_copy():
-        return pltpu.make_async_copy(noise_hbm.at[steps - 1], last_noise, noise_sem.at[steps - 1])
+    def moment_copy(c):
+        return pltpu.make_async_copy(moment_hbm.at[c], moment.at[c], moment_sem.at[0])
+
+    def noise_copy(s, c):
+        return pltpu.make_async_copy(noise_hbm.at[s, c], noise.at[s, c], noise_sem.at[s])
+
+    def obs_copy():
+        return pltpu.make_async_copy(obs_hbm, obs_all, small_sem.at[0])
+
+    def temper_copy():
+        return pltpu.make_async_copy(temper_hbm, temper_ref, small_sem.at[2])
+
+    def inv_copy():
+        return pltpu.make_async_copy(inv_hbm, inv_all, small_sem.at[1])
 
     def spec_copy(s, i, d):
         part = pl.ds(i * chunk_freqs, chunk_freqs)
         return pltpu.make_async_remote_copy(
             src_ref=spec.at[s, freq_peer(d), part],
             dst_ref=field.at[s, part, freq_me],
-            send_sem=spec_send.at[s, d - 1, i],
-            recv_sem=spec_recv.at[s, d - 1, i],
+            send_sem=spec_send.at[0],
+            recv_sem=spec_recv.at[i],
             device_id={"freq": freq_peer(d)},
             device_id_type=MESH,
         )
@@ -103,11 +109,31 @@
         return pltpu.make_async_remote_copy(
             src_ref=src.at[part],
             dst_ref=dst.at[part],
-            send_sem=line_send.at[k, s, i],
-            recv_sem=line_recv.at[k, s, i],
+            send_sem=line_send.at[k],
+            recv_sem=line_recv.at[k, i],
             device_id={"param": peer},
             device_id_type=MESH,
         )
+
+    def spec_arrival(s, i):
+        here = field.at[s, pl.ds(i * chunk_freqs, chunk_freqs), pl.ds(0, freq_count - 1)]
+        return pltpu.make_async_copy(here, here, spec_recv.at[i])
+
+    def spec_departure(s):
+        here = spec.at[s, pl.ds(0, freq_count - 1)]
+        return pltpu.make_async_copy(here, here, spec_send.at[0])
+
+    def adj_arrival(s):
+        here = adj_all.at[s, pl.ds(0, freq_count - 1)]
+        return pltpu.make_async_copy(here, here, adj_recv.at[0])
+
+    def adj_departure(s):
+        here = adj.at[s, :, pl.ds(0, freq_count - 1)]
+        return pltpu.make_async_copy(here, here, adj_send.at[0])
+
+    def line_departure(k, s):
+        here = core_out.at[s]
+        return pltpu.make_async_copy(here, here, line_send.at[k])
 
     def core_reduce(s, i):
         return param_copy(0, s, i, core_out.at[s], core_in.at[s], core_peer)
@@ -126,8 +152,8 @@
         return pltpu.make_async_remote_copy(
             src_ref=adj.at[s, part, freq_peer(d)],
             dst_ref=adj_all.at[s, freq_me, part],
-            send_sem=adj_send.at[s, d - 1, i],
-            recv_sem=adj_recv.at[s, d - 1, i],
+            send_sem=adj_send.at[0],
+            recv_sem=adj_recv.at[0],
             device_id={"freq": freq_peer(d)},
             device_id_type=MESH,
         )
@@ -159,12 +185,9 @@
     def _(c):
         state_copy(c).start()
 
-    for f in range(freq_loc):
-        first = pl.multiple_of(core * half, half)
-        inv_rows[f] = inv_ref[f : f + 1, pl.ds(first, half)]
-        for ri in range(2):
-            first = pl.multiple_of(ri * sensors + core * half, half)
-            obs_rows[f, ri : ri + 1] = obs_ref[f : f + 1, pl.ds(first, half)]
+    obs_copy().start()
+    inv_copy().start()
+    temper_copy().start()
 
     @pl.loop(0, chains_loc)
     def _(c):
@@ -175,14 +198,24 @@
     def _(f):
         green_copy(f).start()
 
-    moment_copy().start()
-    for s in range(steps - 1):
-        noise_copy(s).start()
-    last_noise_copy().start()
+    @pl.loop(0, chains_loc)
+    def _(c):
+        moment_copy(c).start()
+        for s in range(steps - 1):
+            noise_copy(s, c).start()
 
     met = has_above.astype(jnp.int32) + has_below.astype(jnp.int32)
     pl.semaphore_wait(barrier, freq_count + met)
     send_spectrum(0)
+    obs_copy().wait()
+    inv_copy().wait()
+    temper_copy().wait()
+    for f in range(freq_loc):
+        first = pl.multiple_of(core * half, half)
+        inv_rows[f] = inv_all[f : f + 1, pl.ds(first, half)]
+        for ri in range(2):
+            first = pl.multiple_of(ri * sensors + core * half, half)
+            obs_rows[f, ri : ri + 1] = obs_all[f : f + 1, pl.ds(first, half)]
 
     def turned(x, sign):
         wide = x.astype(jnp.float32)
@@ -199,8 +232,7 @@
             for g in range(chunk_freqs):
                 green_copy(i * chunk_freqs + g).wait()
 
-        for d in range(1, freq_count):
-            spec_copy(s, i, d).wait_recv()
+        spec_arrival(s, i).wait()
         for g in range(chunk_freqs):
             f = i * chunk_freqs + g
             x = field[s, f].reshape(all_rows, slab)
@@ -316,18 +348,27 @@
             stage(0, forward)
             stage(weigh_lag + GATHER_LAG, backward)
 
-        @pl.loop(0, chunks)
-        def _(i):
-            for d in range(1, freq_count):
-                adj_copy(s, i, d).wait_recv()
+        adj_arrival(s).wait()
+        spec_departure(s).wait()
+        adj_departure(s).wait()
+        for k in range(2):
+            line_departure(k, s).wait()
+
+        @pl.when(has_above)
+        def _():
+            line_departure(2, s).wait()
+
+        @pl.when(has_below)
+        def _():
+            line_departure(3, s).wait()
 
         @pl.when(s < steps - 1)
         def _():
             @pl.when(s == 0)
             def _():
-                moment_copy().wait()
-
-            noise_copy(s).wait()
+                pltpu.make_async_copy(moment, moment, moment_sem.at[0]).wait()
+
+            pltpu.make_async_copy(noise.at[s], noise.at[s], noise_sem.at[s]).wait()
 
             @pl.loop(0, freq_count)
             def _(j):
@@ -348,26 +389,6 @@
                 transform(c, current.astype(jnp.bfloat16))
 
             send_spectrum(s + 1)
-
-    last_noise_copy().wait()
-
-    @pl.loop(0, steps)
-    def _(s):
-        @pl.loop(0, chunks)
-        def _(i):
-            for d in range(1, freq_count):
-                spec_copy(s, i, d).wait_send()
-                adj_copy(s, i, d).wait_send()
-            core_reduce(s, i).wait_send()
-            core_gather(s, i).wait_send()
-
-            @pl.when(has_above)
-            def _():
-                up_copy(s, i).wait_send()
-
-            @pl.when(has_below)
-            def _():
-                down_copy(s, i).wait_send()
 
 
 def advance(c, rows32, table_ref, temper_ref, current, spread, push):
@@ -392,8 +413,8 @@
 
 
 def final_kernel(
-    table_ref, temper_ref, adj_all, state, moment, push, state_hbm, moment_hbm,
-    rows32, new_state, new_moment, state_sem, moment_sem,
+    table_ref, temper_ref, adj_all, state, moment, noise_hbm, state_hbm, moment_hbm,
+    rows32, push, new_state, new_moment, push_sem, state_sem, moment_sem,
 ):
     last = adj_all.shape[0] - 1
     freq_count, freq_loc, rows, slab = adj_all.shape[1:]
@@ -403,6 +424,13 @@
 
     def moment_copy(c):
         return pltpu.make_async_copy(new_moment.at[c], moment_hbm.at[c], moment_sem.at[c])
+
+    def push_copy(c):
+        return pltpu.make_async_copy(noise_hbm.at[last, c], push.at[c], push_sem.at[c])
+
+    @pl.loop(0, state.shape[0])
+    def _(c):
+        push_copy(c).start()
 
     @pl.loop(0, freq_count)
     def _(j):
@@ -414,6 +442,7 @@
 
     @pl.loop(0, state.shape[0])
     def _(c):
+        push_copy(c).wait()
         current, spread = advance(
             c, rows32, table_ref, temper_ref, state[c], moment[c], push[c]
         )
@@ -459,18 +488,19 @@
     hbm = pl.BlockSpec(memory_space=pltpu.HBM)
     line_buf = pltpu.VMEM((steps, freq_loc, all_rows, half), bf16)
     rows32 = pltpu.VMEM((slab // LANES, columns * chains_loc, LANES), f32)
-    peers = freq_count - 1
-    adj_all, state, moment, push = pl.pallas_call(
+    adj_all, state, moment = pl.pallas_call(
         functools.partial(steps_kernel, freq_count, param_count, CHUNK_FREQS),
         out_shape=[
             jax.ShapeDtypeStruct((steps, freq_count, freq_loc, rows, slab), bf16),
             jax.ShapeDtypeStruct(chain_state.shape, f32),
             jax.ShapeDtypeStruct(chain_state.shape, f32),
-            jax.ShapeDtypeStruct(chain_state.shape, f32),
         ],
-        in_specs=[vmem, smem, vmem, vmem, hbm, hbm, hbm, hbm],
-        out_specs=[vmem, vmem, vmem, vmem],
+        in_specs=[vmem, hbm, hbm, hbm, hbm, hbm, hbm, hbm],
+        out_specs=[vmem, vmem, vmem],
         scratch_shapes=[
+            pltpu.SMEM(temper.shape, f32),
+            pltpu.VMEM(observed.shape, f32),
+            pltpu.VMEM(inv_noise.shape, f32),
             pltpu.VMEM((freq_loc, 2, half), f32),
             pltpu.VMEM((freq_loc, 1, half), f32),
             pltpu.VMEM((freq_loc, 2, slab, sensors), bf16),
@@ -482,16 +512,17 @@
             line_buf, line_buf, line_buf, line_buf, line_buf, line_buf,
             pltpu.VMEM((steps, 2, freq_loc, all_rows, half), bf16),
             pltpu.VMEM((steps, freq_loc, freq_count, rows, slab), bf16),
+            dma((3,)),
             dma((chains_loc,)),
             dma((freq_loc,)),
             dma((1,)),
-            dma((steps,)),
-            dma((steps, peers, chunks)),
-            dma((steps, peers, chunks)),
-            dma((4, steps, chunks)),
-            dma((4, steps, chunks)),
-            dma((steps, peers, chunks)),
-            dma((steps, peers, chunks)),
+            dma((max(steps - 1, 1),)),
+            dma((1,)),
+            dma((chunks,)),
+            dma((4,)),
+            dma((4, chunks)),
+            dma((1,)),
+            dma((1,)),
         ],
         compiler_params=pltpu.CompilerParams(
             collective_id=0, has_side_effects=True, vmem_limit_bytes=44 * 2**20
@@ -503,17 +534,19 @@
             jax.ShapeDtypeStruct(chain_state.shape, f32),
             jax.ShapeDtypeStruct(chain_state.shape, f32),
         ],
-        in_specs=[vmem, smem, vmem, vmem, vmem, vmem],
+        in_specs=[vmem, smem, vmem, vmem, vmem, hbm],
         out_specs=[hbm, hbm],
         scratch_shapes=[
             rows32,
             pltpu.VMEM(chain_state.shape, f32),
             pltpu.VMEM(chain_state.shape, f32),
+            pltpu.VMEM(chain_state.shape, f32),
+            dma((chains_loc,)),
             dma((chains_loc,)),
             dma((chains_loc,)),
         ],
-        compiler_params=pltpu.CompilerParams(vmem_limit_bytes=14 * 2**20),
-    )(table, temper, adj_all, state, moment, push)
+        compiler_params=pltpu.CompilerParams(vmem_limit_bytes=18 * 2**20),
+    )(table, temper, adj_all, state, moment, noise)
 
 
 def on_device(chain_state, second_moment, noise, green, observed, inv_noise, temper):

time: 95.1 us -> 80.6 us (0.85)
  Pallas kernels: 88.9 us -> 76.3 us
  local copies, waits for them, and re-layouts: 4.62 us -> 2.85 us
    pallas_call x1, Pallas kernels: 83.5 us -> 70.5 us  [kernel_steps(): pl.pallas_call(functools.partial(steps_kernel, freq_count, param_count, C...]
    unnamed x8 -> x10, local copies, waits for them, and re-layouts: 4.43 us -> 2.66 us
where the time goes in v2:
time: 80.6 us; the launch traced here: 80.5 us
  Pallas kernels  76.3 us (95%)
  local copies, waits for them, and re-layouts  2.85 us (4%)
    pallas_call x1, Pallas kernels, kernel_steps(): pl.pallas_call(functools.partial(steps_kernel, freq_count, param_count, C...  70.5 us
    pallas_call x1, Pallas kernels, kernel_steps(): pl.pallas_call(final_kernel, out_shape=[jax.ShapeDtypeStruct(chain_state....  5.73 us
    unnamed x10, local copies, waits for them, and re-layouts  2.66 us

profile of v2, /device:TPU:0, one launch (start us, length us, event | category | flops | bytes accessed | tf_op | source)
XLA Modules:
  0.0 80.5 jit_solution(2003207502790142501)
XLA Ops:
  0.6 0.6 fusion.7
  1.3 0.1 copy.9
  1.4 0.1 convert_element_type.24
  1.5 0.0 slice-start
  1.5 0.0 copy-start
  1.5 1.0 %copy-done = f32[16,1024]{1,0:T(8,128)S(1)} copy-done((f32[16,1024]{1,0:T(8,128)S(1)}, f32[16,1024]{1,0:T(8,128)}, u32[]{:S(2)}) %copy-start) | copy-done | bytes 65560
  2.5 0.0 copy-start.1
  2.5 1.0 %copy-done.1 = f32[16,512]{1,0:T(8,128)S(1)} copy-done((f32[16,512]{1,0:T(8,128)S(1)}, f32[16,512]{1,0:T(8,128)}, u32[]{:S(2)}) %copy-start.1) | copy-done | bytes 32792
  3.5 0.0 copy-start.2
  3.5 0.7 copy-done.2
  4.1 0.0 slice-start.1
  4.1 70.5 %shard_map.86 = (bf16[2,4,16,16,256]{4,3,2,1,0:T(8,128)(2,1)S(1)}, f32[8,256,512]{2,1,0:T(8,128)S(1)}, f32[8,256,512]{2,1,0:T(8,128)S(1)}) custom-call(bf16[128,512]{1,0:T(8,128)(2,1)S(1)} %bitcast.5, f32[8]{0:T(128)S(1)} %copy-done.2, f32[16,1024]{1,0:T(8,128)S(1)} %copy-done, f32[16,512]{1,0:T(8,128)S(1)} %copy-done.1, f32[8,256,512]{2,1,0:T(8,128)} %state_hbm.1, ...), custom_call_target="tpu_custom_call" | custom-call | tf_op jit(solution)/shard_map/pallas_call | solution.py:491
  74.7 0.0 slice-done
  74.7 0.0 slice-done.1
  74.7 5.7 %shard_map.87 = (f32[8,256,512]{2,1,0:T(8,128)}, f32[8,256,512]{2,1,0:T(8,128)}) custom-call(bf16[128,512]{1,0:T(8,128)(2,1)S(1)} %bitcast.6, f32[8]{0:T(128)S(1)} %copy-done.2, bf16[2,4,16,16,256]{4,3,2,1,0:T(8,128)(2,1)S(1)} %get-tuple-element.5.adj_all, f32[8,256,512]{2,1,0:T(8,128)S(1)} %get-tuple-element.6.state, ...), custom_call_target="tpu_custom_call" | custom-call | tf_op jit(solution)/shard_map/pallas_call | solution.py:531
  (3 shorter events, 0.0 us)
Async XLA Ops:
  1.5 73.2 %slice-start = ((s8[8388608]{0:T(1024)(128)(4,1)}), s8[4194304]{0:T(1024)(128)(4,1)S(1)}, s32[]{:S(2)}) async-start(s8[8388608]{0:T(1024)(128)(4,1)} %bitcast.3), calls=%async_computation | async-start | bytes 8388608
  1.5 1.0 %copy-start = (f32[16,1024]{1,0:T(8,128)S(1)}, f32[16,1024]{1,0:T(8,128)}, u32[]{:S(2)}) copy-start(f32[16,1024]{1,0:T(8,128)} %obs_hbm.1) | copy-start | bytes 196612
  2.5 1.0 %copy-start.1 = (f32[16,512]{1,0:T(8,128)S(1)}, f32[16,512]{1,0:T(8,128)}, u32[]{:S(2)}) copy-start(f32[16,512]{1,0:T(8,128)} %inv_hbm.1) | copy-start | bytes 98308
  3.5 0.7 copy-start.2
  4.1 70.6 %slice-start.1 = ((s8[8388608]{0:T(1024)(128)(4,1)}), s8[4194304]{0:T(1024)(128)(4,1)S(1)}, s32[]{:S(2)}) async-start(s8[8388608]{0:T(1024)(128)(4,1)} %bitcast.3), calls=%async_computation.1 | async-start | bytes 8388608

commit v3 on v2

v3 whole, which is shorter than its diff:
```python
import functools
import math

import jax
import jax.numpy as jnp
from jax import lax
from jax.experimental import pallas as pl
from jax.experimental.pallas import tpu as pltpu
from jax.sharding import PartitionSpec as P

decay_rate = 0.9
step_length = 0.5
MESH = pl.DeviceIdType.MESH
LANES = 128
GROUPS = 2
CHUNK_FREQS = 2
CORE_LAG = 2
HOP_LAG = 5
GATHER_LAG = 3
ADJ_LAG = 8
SPEC_LAG = 9


def spectral_table(time_len, freq_total):
    time_index = jnp.arange(time_len, dtype=jnp.int32)[:, None]
    wave_number = jnp.arange(freq_total, dtype=jnp.int32)[None, :] + 1
    phase_angle = (time_index * wave_number % time_len).astype(jnp.float32) * (
        2.0 * math.pi / time_len
    )
    columns_table = jnp.stack([jnp.cos(phase_angle), -jnp.sin(phase_angle)], axis=-1).reshape(
        time_len, 2 * freq_total
    )
    return (columns_table / math.sqrt(time_len)).astype(jnp.bfloat16)


def steps_kernel(
    freq_count, param_count, chunk_freqs,
    table_ref, temper_hbm, obs_hbm, inv_hbm, state_hbm, moment_hbm, noise_hbm, green_hbm,
    adj_all, state, moment,
    temper_ref, obs_all, inv_all, obs_rows, inv_rows, green, noise, rows32, spec, field, acc,
    core_out, core_in, up_out, up_in, down_out, down_in, wtd, adj,
    small_sem, state_sem, green_sem, moment_sem, noise_sem, spec_send, spec_recv,
    line_send, line_recv, adj_send, adj_recv,
):
    freq_me = lax.axis_index("freq")
    param_me = lax.axis_index("param")
    steps = noise.shape[0]
    groups = acc.shape[0]
    freq_loc = field.shape[1]
    rows, slab = field.shape[3], field.shape[4]
    group_chains = rows // 2
    all_rows, half = acc.shape[2], acc.shape[3]
    sensors = 2 * half
    col_blocks = slab // LANES
    columns = table_ref.shape[0]
    chunks = freq_loc // chunk_freqs
    line = param_count // 2
    core = lax.rem(param_me, 2)
    chip = param_me // 2
    core_peer = param_me + 1 - 2 * core
    above, below = param_me + 2, param_me - 2
    has_above, has_below = chip < line - 1, chip > 0
    peers = pl.ds(0, freq_count - 1)

    def freq_peer(d):
        return lax.rem(freq_me + d, freq_count)

    barrier = pltpu.get_barrier_semaphore()
    for d in range(1, freq_count):
        pl.semaphore_signal(barrier, inc=1, device_id={"freq": freq_peer(d)}, device_id_type=MESH)
    pl.semaphore_signal(barrier, inc=1, device_id={"param": core_peer}, device_id_type=MESH)

    @pl.when(has_above)
    def _():
        pl.semaphore_signal(barrier, inc=1, device_id={"param": above}, device_id_type=MESH)

    @pl.when(has_below)
    def _():
        pl.semaphore_signal(barrier, inc=1, device_id={"param": below}, device_id_type=MESH)

    def state_copy(c):
        return pltpu.make_async_copy(state_hbm.at[c], state.at[c], state_sem.at[c])

    def green_copy(f):
        return pltpu.make_async_copy(green_hbm.at[:, f], green.at[f], green_sem.at[f])

    def moment_copy(c):
        return pltpu.make_async_copy(moment_hbm.at[c], moment.at[c], moment_sem.at[0])

    def noise_copy(s, c):
        return pltpu.make_async_copy(noise_hbm.at[s, c], noise.at[s, c], noise_sem.at[s])

    def small_copy(k, src, dst):
        return pltpu.make_async_copy(src, dst, small_sem.at[k])

    def arrived(ref, sem):
        pltpu.make_async_copy(ref, ref, sem).wait()

    def freqs_of(i):
        return pl.ds(i * chunk_freqs, chunk_freqs)

    def spec_copy(q, g, i, d):
        return pltpu.make_async_remote_copy(
            src_ref=spec.at[q, freq_peer(d), freqs_of(i)],
            dst_ref=field.at[q, freqs_of(i), freq_me],
            send_sem=spec_send.at[0],
            recv_sem=spec_recv.at[g, i],
            device_id={"freq": freq_peer(d)},
            device_id_type=MESH,
        )

    def adj_copy(q, g, i, d):
        return pltpu.make_async_remote_copy(
            src_ref=adj.at[q, freqs_of(i), freq_peer(d)],
            dst_ref=adj_all.at[q, freq_me, freqs_of(i)],
            send_sem=adj_send.at[0],
            recv_sem=adj_recv.at[g],
            device_id={"freq": freq_peer(d)},
            device_id_type=MESH,
        )

    def param_copy(k, g, i, src, dst, peer):
        return pltpu.make_async_remote_copy(
            src_ref=src.at[freqs_of(i)],
            dst_ref=dst.at[freqs_of(i)],
            send_sem=line_send.at[k],
            recv_sem=line_recv.at[k, g, i],
            device_id={"param": peer},
            device_id_type=MESH,
        )

    def core_reduce(q, g, i):
        return param_copy(0, g, i, core_out.at[q], core_in.at[q], core_peer)

    def core_gather(q, g, i):
        return param_copy(1, g, i, wtd.at[q, core], wtd.at[q, core], core_peer)

    def up_copy(q, g, i):
        return param_copy(2, g, i, up_out.at[q], up_in.at[q], above)

    def down_copy(q, g, i):
        return param_copy(3, g, i, down_out.at[q], down_in.at[q], below)

    def transform(g, k, low):
        dims = (((1,), (1,)), ((), ()))
        result = lax.dot_general(table_ref[...], low, dims, preferred_element_type=jnp.float32)
        for b in range(col_blocks):
            block = result[:, b * LANES : (b + 1) * LANES]
            rows32[g, b, pl.ds(k, columns, stride=group_chains)] = block

    def send_spectrum(q, g):
        @pl.loop(0, chunks)
        def _(i):
            for d in range(freq_count):
                for e in range(chunk_freqs):
                    f = i * chunk_freqs + e
                    first = pl.multiple_of((freq_peer(d) * freq_loc + f) * rows, rows)
                    pieces = [rows32[g, b, pl.ds(first, rows)] for b in range(col_blocks)]
                    tile = jnp.concatenate(pieces, axis=1).astype(jnp.bfloat16)
                    if d == 0:
                        field[q, f, freq_me] = tile
                    else:
                        spec[q, freq_peer(d), f] = tile
            for d in range(1, freq_count):
                spec_copy(q, g, i, d).start()

    @pl.loop(0, groups * group_chains)
    def _(c):
        state_copy(c).start()

    smalls = ((temper_hbm, temper_ref), (obs_hbm, obs_all), (inv_hbm, inv_all))
    for k, (src, dst) in enumerate(smalls):
        small_copy(k, src, dst).start()

    met = has_above.astype(jnp.int32) + has_below.astype(jnp.int32)
    for g in range(groups):
        @pl.loop(0, group_chains)
        def _(k):
            c = g * group_chains + k
            state_copy(c).wait()
            transform(g, k, state[c].astype(jnp.bfloat16))

        if g == groups - 1:
            @pl.loop(0, freq_loc)
            def _(f):
                green_copy(f).start()

            @pl.loop(0, groups * group_chains)
            def _(c):
                moment_copy(c).start()
                for s in range(steps):
                    noise_copy(s, c).start()

        if g == 0:
            pl.semaphore_wait(barrier, freq_count + met)
        send_spectrum(g, g)

    for k, (src, dst) in enumerate(smalls):
        small_copy(k, src, dst).wait()
    for f in range(freq_loc):
        first = pl.multiple_of(core * half, half)
        inv_rows[f] = inv_all[f : f + 1, pl.ds(first, half)]
        for ri in range(2):
            first = pl.multiple_of(ri * sensors + core * half, half)
            target = obs_all[f : f + 1, pl.ds(first, half)]
            obs_rows[f, ri * group_chains : (ri + 1) * group_chains] = jnp.broadcast_to(
                target, (group_chains, half)
            )

    def turned(x, sign):
        wide = x.astype(jnp.float32).reshape(freq_count, rows, x.shape[-1])
        row = lax.broadcasted_iota(jnp.int32, wide.shape, 1)
        back = pltpu.roll(wide, group_chains, 1)
        flip = row < group_chains if sign > 0 else row >= group_chains
        return jnp.where(flip, -back, back).reshape(all_rows, x.shape[-1]).astype(jnp.bfloat16)

    def forward(s, n):
        g, i = lax.div(n, chunks), lax.rem(n, chunks)
        q = s * groups + g

        @pl.when((s == 0) & (g == 0))
        def _():
            for e in range(chunk_freqs):
                green_copy(i * chunk_freqs + e).wait()

        arrived(field.at[q, freqs_of(i), peers], spec_recv.at[g, i])
        for e in range(chunk_freqs):
            f = i * chunk_freqs + e
            wide = field[q, f].astype(jnp.float32).reshape(all_rows, slab)
            both = jnp.concatenate([wide.astype(jnp.bfloat16), turned(wide, 1)], axis=1)
            weights = green[f].reshape(2 * slab, sensors)
            data = jnp.dot(both, weights, preferred_element_type=jnp.float32)
            low, high = data[:, :half], data[:, half:]
            acc[g, f] = jnp.where(core == 0, low, high)
            core_out[q, f] = jnp.where(core == 0, high, low).astype(jnp.bfloat16)
        core_reduce(q, g, i).start()

    def merge(s, n):
        g, i = lax.div(n, chunks), lax.rem(n, chunks)
        q = s * groups + g
        core_reduce(q, g, i).wait_recv()
        total = acc[g, freqs_of(i)] + core_in[q, freqs_of(i)].astype(jnp.float32)
        acc[g, freqs_of(i)] = total

        @pl.when(chip == 0)
        def _():
            up_out[q, freqs_of(i)] = total.astype(jnp.bfloat16)
            up_copy(q, g, i).start()

        @pl.when(chip == line - 1)
        def _():
            down_out[q, freqs_of(i)] = total.astype(jnp.bfloat16)
            down_copy(q, g, i).start()

    def pass_up(s, n):
        g, i = lax.div(n, chunks), lax.rem(n, chunks)
        q = s * groups + g
        up_copy(q, g, i).wait_recv()
        total = acc[g, freqs_of(i)] + up_in[q, freqs_of(i)].astype(jnp.float32)
        up_out[q, freqs_of(i)] = total.astype(jnp.bfloat16)
        up_copy(q, g, i).start()

    def pass_down(s, n):
        g, i = lax.div(n, chunks), lax.rem(n, chunks)
        q = s * groups + g
        down_copy(q, g, i).wait_recv()
        total = acc[g, freqs_of(i)] + down_in[q, freqs_of(i)].astype(jnp.float32)
        down_out[q, freqs_of(i)] = total.astype(jnp.bfloat16)
        down_copy(q, g, i).start()

    def weigh(s, n):
        g, i = lax.div(n, chunks), lax.rem(n, chunks)
        q = s * groups + g

        @pl.when(chip == line - 1)
        def _():
            up_copy(q, g, i).wait_recv()

        @pl.when(chip == 0)
        def _():
            down_copy(q, g, i).wait_recv()

        @pl.when(has_below)
        def _():
            acc[g, freqs_of(i)] += up_in[q, freqs_of(i)].astype(jnp.float32)

        @pl.when(has_above)
        def _():
            acc[g, freqs_of(i)] += down_in[q, freqs_of(i)].astype(jnp.float32)

        for e in range(chunk_freqs):
            f = i * chunk_freqs + e
            apart = acc[g, f].reshape(freq_count, rows, half) - obs_rows[f][None]
            scaled = inv_rows[f][None] * apart
            wtd[q, core, f] = scaled.reshape(all_rows, half).astype(jnp.bfloat16)
        core_gather(q, g, i).start()

    def backward(s, n):
        g, i = lax.div(n, chunks), lax.rem(n, chunks)
        q = s * groups + g
        core_gather(q, g, i).wait_recv()
        dims = (((1,), (1,)), ((), ()))
        for e in range(chunk_freqs):
            f = i * chunk_freqs + e
            w = jnp.concatenate([wtd[q, 0, f], wtd[q, 1, f]], axis=1)
            first = lax.dot_general(w, green[f, 0], dims, preferred_element_type=jnp.float32)
            second = lax.dot_general(
                turned(w, -1), green[f, 1], dims, preferred_element_type=jnp.float32
            )
            back = (first + second).reshape(freq_count, rows, slab)
            adj[q, f] = back.astype(jnp.bfloat16)
            adj_all[q, freq_me, f] = adj[q, f, freq_me]
        for d in range(1, freq_count):
            adj_copy(q, g, i, d).start()

    def update(s, n):
        g, k = lax.div(n, chunks), lax.rem(n, chunks)
        q = s * groups + g
        going_on = s < steps - 1

        @pl.when((k < group_chains) & (going_on | (g < groups - 1)))
        def _():
            @pl.when(k == 0)
            def _():
                arrived(adj_all.at[q, peers], adj_recv.at[g])
                widen(adj_all.at[q], rows32.at[g])

                @pl.when(g == 0)
                def _():
                    @pl.when(s == 0)
                    def _():
                        arrived(moment, moment_sem.at[0])

                    arrived(noise.at[s], noise_sem.at[s])

            c = g * group_chains + k
            low = advance(
                k, c, rows32.at[g], table_ref, temper_ref, state, moment, noise.at[s], state, moment
            )

            @pl.when(going_on)
            def _():
                transform(g, k, low)

            @pl.when(going_on & (k == group_chains - 1))
            def _():
                send_spectrum(q + groups, g)

    span = groups * chunks
    up_lag = CORE_LAG + HOP_LAG * chip
    down_lag = CORE_LAG + HOP_LAG * (line - 1 - chip)
    weigh_lag = jnp.maximum(up_lag, down_lag)
    back_lag = CORE_LAG + HOP_LAG * (line - 1) + GATHER_LAG
    update_lag = back_lag + chunks - 1 + ADJ_LAG
    period = max(update_lag + group_chains - 1 + SPEC_LAG, span)
    inside = has_above & has_below
    total_ticks = (steps - 1) * period + max(
        span + back_lag, update_lag + (groups - 2) * chunks + group_chains
    )

    @pl.loop(0, total_ticks)
    def _(tick):
        def stage(lag, work, allowed=None):
            since = jnp.maximum(tick - lag, 0)
            s = lax.div(since, period)
            n = since - s * period
            due = (tick >= lag) & (s < steps) & (n < span)

            @pl.when(due if allowed is None else due & allowed)
            def _():
                work(s, n)

        stage(0, forward)
        stage(weigh_lag + GATHER_LAG, backward)
        stage(CORE_LAG, merge)
        stage(up_lag, pass_up, inside)
        stage(down_lag, pass_down, inside)
        stage(weigh_lag, weigh)
        stage(update_lag, update)

    last = steps * groups - 1
    arrived(adj_all.at[last, peers], adj_recv.at[groups - 1])
    arrived(spec.at[:, peers], spec_send.at[0])
    arrived(adj.at[:, :, peers], adj_send.at[0])
    for k in range(2):
        arrived(core_out, line_send.at[k])

    @pl.when(has_above)
    def _():
        arrived(core_out, line_send.at[2])

    @pl.when(has_below)
    def _():
        arrived(core_out, line_send.at[3])


def widen(adj, rows32):
    freq_count, freq_loc, rows, slab = adj.shape

    @pl.loop(0, freq_count)
    def _(j):
        for f in range(freq_loc):
            first = pl.multiple_of((j * freq_loc + f) * rows, rows)
            tile = adj[j, f].astype(jnp.float32)
            for b in range(slab // LANES):
                rows32[b, pl.ds(first, rows)] = tile[:, b * LANES : (b + 1) * LANES]


def advance(k, c, rows32, table_ref, temper_ref, state, moment, push, new_state, new_moment):
    columns, group_chains = table_ref.shape[0], rows32.shape[1] // table_ref.shape[0]
    pieces = [
        rows32[b, pl.ds(k, columns, stride=group_chains)] for b in range(rows32.shape[0])
    ]
    mine = jnp.concatenate(pieces, axis=1).T.astype(jnp.bfloat16)
    gradient = jnp.dot(mine, table_ref[...], preferred_element_type=jnp.float32)
    current = state[c]
    drift_term = temper_ref[c] * gradient + current
    spread = moment[c]
    spread = decay_rate * spread + (1.0 - decay_rate) * drift_term * drift_term
    precondition = lax.rsqrt(spread)
    root = precondition * lax.rsqrt(precondition)
    current = (
        current
        - step_length * precondition * drift_term
        + math.sqrt(2.0 * step_length) * root * push[c]
    )
    new_state[c] = current
    new_moment[c] = spread
    return current.astype(jnp.bfloat16)


def final_kernel(
    table_ref, temper_ref, adj_all, state, moment, noise_hbm, state_hbm, moment_hbm,
    rows32, push, new_state, new_moment, push_sem, state_sem, moment_sem,
):
    last, step = adj_all.shape[0] - 1, noise_hbm.shape[0] - 1
    left = new_state.shape[0]
    done = state.shape[0] - left

    def push_copy(k):
        return pltpu.make_async_copy(noise_hbm.at[step, done + k], push.at[k], push_sem.at[k])

    def state_copy(k):
        c = done + k
        return pltpu.make_async_copy(new_state.at[k], state_hbm.at[c], state_sem.at[c])

    def moment_copy(k):
        c = done + k
        return pltpu.make_async_copy(new_moment.at[k], moment_hbm.at[c], moment_sem.at[c])

    def done_state_copy(c):
        return pltpu.make_async_copy(state.at[c], state_hbm.at[c], state_sem.at[c])

    def done_moment_copy(c):
        return pltpu.make_async_copy(moment.at[c], moment_hbm.at[c], moment_sem.at[c])

    @pl.loop(0, left)
    def _(k):
        push_copy(k).start()

    @pl.loop(0, done)
    def _(c):
        done_state_copy(c).start()
        done_moment_copy(c).start()

    widen(adj_all.at[last], rows32)

    @pl.loop(0, left)
    def _(k):
        push_copy(k).wait()
        advance(
            k, k, rows32, table_ref, temper_ref.at[pl.ds(done, left)], state.at[pl.ds(done, left)],
            moment.at[pl.ds(done, left)], push, new_state, new_moment,
        )
        state_copy(k).start()
        moment_copy(k).start()

    @pl.loop(0, done)
    def _(c):
        done_state_copy(c).wait()
        done_moment_copy(c).wait()

    @pl.loop(0, left)
    def _(k):
        state_copy(k).wait()
        moment_copy(k).wait()


def fits_kernel(chain_shape, green_shape):
    chains_loc, slab = chain_shape[0], chain_shape[1]
    param_count = lax.axis_size("param")
    return (
        chains_loc % GROUPS == 0
        and 2 * (chains_loc // GROUPS) % 8 == 0
        and slab % LANES == 0
        and chain_shape[2] % LANES == 0
        and green_shape[3] % (2 * LANES) == 0
        and green_shape[1] % CHUNK_FREQS == 0
        and green_shape[1] // CHUNK_FREQS >= chains_loc // GROUPS
        and param_count == 8
        and lax.axis_size("freq") > 1
    )


def kernel_steps(chain_state, second_moment, noise, green, observed, inv_noise, temper):
    chains_loc, slab, time_len = chain_state.shape
    freq_loc, sensors = green.shape[1], green.shape[3]
    steps = noise.shape[0]
    freq_count, param_count = lax.axis_size("freq"), lax.axis_size("param")
    columns = 2 * freq_loc * freq_count
    table = spectral_table(time_len, freq_loc * freq_count).T
    chunks = freq_loc // CHUNK_FREQS
    group_chains = chains_loc // GROUPS
    rows, half = 2 * group_chains, sensors // 2
    all_rows = freq_count * rows
    items = steps * GROUPS
    bf16, f32 = jnp.bfloat16, jnp.float32
    dma = pltpu.SemaphoreType.DMA
    vmem = pl.BlockSpec(memory_space=pltpu.VMEM)
    smem = pl.BlockSpec(memory_space=pltpu.SMEM)
    hbm = pl.BlockSpec(memory_space=pltpu.HBM)
    line_buf = pltpu.VMEM((items, freq_loc, all_rows, half), bf16)
    rows32 = (slab // LANES, columns * group_chains, LANES)
    part = (group_chains, slab, time_len)
    observed, inv_noise, temper_hbm, noise = (
        pltpu.with_memory_space_constraint(x, pltpu.HBM)
        for x in (observed, inv_noise, temper, noise)
    )
    adj_all, state, moment = pl.pallas_call(
        functools.partial(steps_kernel, freq_count, param_count, CHUNK_FREQS),
        out_shape=[
            jax.ShapeDtypeStruct((items, freq_count, freq_loc, rows, slab), bf16),
            jax.ShapeDtypeStruct(chain_state.shape, f32),
            jax.ShapeDtypeStruct(chain_state.shape, f32),
        ],
        in_specs=[vmem, hbm, hbm, hbm, hbm, hbm, hbm, hbm],
        out_specs=[vmem, vmem, vmem],
        scratch_shapes=[
            pltpu.SMEM(temper.shape, f32),
            pltpu.VMEM(observed.shape, f32),
            pltpu.VMEM(inv_noise.shape, f32),
            pltpu.VMEM((freq_loc, rows, half), f32),
            pltpu.VMEM((freq_loc, 1, half), f32),
            pltpu.VMEM((freq_loc, 2, slab, sensors), bf16),
            pltpu.VMEM((steps,) + chain_state.shape, f32),
            pltpu.VMEM((GROUPS,) + rows32, f32),
            pltpu.VMEM((items, freq_count, freq_loc, rows, slab), bf16),
            pltpu.VMEM((items, freq_loc, freq_count, rows, slab), bf16),
            pltpu.VMEM((GROUPS, freq_loc, all_rows, half), f32),
            line_buf, line_buf, line_buf, line_buf, line_buf, line_buf,
            pltpu.VMEM((items, 2, freq_loc, all_rows, half), bf16),
            pltpu.VMEM((items, freq_loc, freq_count, rows, slab), bf16),
            dma((3,)),
            dma((chains_loc,)),
            dma((freq_loc,)),
            dma((1,)),
            dma((steps,)),
            dma((1,)),
            dma((GROUPS, chunks)),
            dma((4,)),
            dma((4, GROUPS, chunks)),
            dma((1,)),
            dma((GROUPS,)),
        ],
        compiler_params=pltpu.CompilerParams(
            collective_id=0, has_side_effects=True, vmem_limit_bytes=44 * 2**20
        ),
    )(table, temper_hbm, observed, inv_noise, chain_state, second_moment, noise, green)
    return pl.pallas_call(
        final_kernel,
        out_shape=[
            jax.ShapeDtypeStruct(chain_state.shape, f32),
            jax.ShapeDtypeStruct(chain_state.shape, f32),
        ],
        in_specs=[vmem, smem, vmem, vmem, vmem, hbm],
        out_specs=[hbm, hbm],
        scratch_shapes=[
            pltpu.VMEM(rows32, f32),
            pltpu.VMEM(part, f32),
            pltpu.VMEM(part, f32),
            pltpu.VMEM(part, f32),
            dma((group_chains,)),
            dma((chains_loc,)),
            dma((chains_loc,)),
        ],
        compiler_params=pltpu.CompilerParams(vmem_limit_bytes=18 * 2**20),
    )(table, temper, adj_all, state, moment, noise)


def on_device(chain_state, second_moment, noise, green, observed, inv_noise, temper):
    if fits_kernel(chain_state.shape, green.shape):
        return kernel_steps(
            chain_state, second_moment, noise, green, observed, inv_noise, temper
        )
    chains_loc, slab_rows, time_len = chain_state.shape
    freq_loc = green.shape[1]
    freq_count = lax.axis_size("freq")
    freq_total = freq_loc * freq_count
    chains = chains_loc * freq_count
    forward_table = spectral_table(time_len, freq_total)
    inverse_table = forward_table.T
    green_re = green[0]
    green_im = green[1]
    upper_rows = jnp.concatenate([green_re, green_im], axis=2)
    lower_rows = jnp.concatenate([-green_im, green_re], axis=2)
    kernel = jnp.concatenate([upper_rows, lower_rows], axis=1)
    weights = jnp.concatenate([inv_noise, inv_noise], axis=1)
    temper_cols = temper[:, None, None]
    current = chain_state
    moment = second_moment
    for step_num in range(noise.shape[0]):
        low_state = current.astype(jnp.bfloat16)
        local_spec = jnp.dot(
            low_state.reshape(chains_loc * slab_rows, time_len),
            forward_table,
            preferred_element_type=jnp.float32,
        )
        local_spec = local_spec.astype(jnp.bfloat16).reshape(chains_loc, slab_rows, 2 * freq_total)
        spectrum = lax.all_to_all(local_spec, "freq", split_axis=2, concat_axis=0, tiled=True)
        mixed_spec = (
            spectrum.reshape(chains, slab_rows, freq_loc, 2)
            .transpose(2, 0, 3, 1)
            .reshape(freq_loc, chains, 2 * slab_rows)
        )
        partial_data = jnp.einsum(
            "fcq,fqs->fcs", mixed_spec, kernel, preferred_element_type=jnp.float32
        )
        predicted = lax.psum(partial_data.astype(jnp.bfloat16), "param").astype(jnp.float32)
        weighted = (weights[:, None, :] * (predicted - observed[:, None, :])).astype(jnp.bfloat16)
        adjoint = jnp.einsum(
            "fcs,fqs->fcq", weighted, kernel, preferred_element_type=jnp.float32
        ).astype(jnp.bfloat16)
        adjoint = (
            adjoint.reshape(freq_loc, chains, 2, slab_rows)
            .transpose(1, 3, 0, 2)
            .reshape(chains, slab_rows, 2 * freq_loc)
        )
        own_adjoint = lax.all_to_all(adjoint, "freq", split_axis=0, concat_axis=2, tiled=True)
        gradient = jnp.dot(
            own_adjoint.reshape(chains_loc * slab_rows, 2 * freq_total),
            inverse_table,
            preferred_element_type=jnp.float32,
        )
        gradient = gradient.reshape(chains_loc, slab_rows, time_len)
        drift_term = temper_cols * gradient + current
        moment = decay_rate * moment + (1.0 - decay_rate) * drift_term * drift_term
        precondition = lax.rsqrt(moment)
        current = (
            current
            - step_length * precondition * drift_term
            + math.sqrt(2.0 * step_length) * jnp.sqrt(precondition) * noise[step_num]
        )
    return (current, moment)


def solution(mesh):
    return jax.shard_map(
        on_device,
        mesh=mesh,
        in_specs=(
            P("freq", "param", None),
            P("freq", "param", None),
            P(None, "freq", "param", None),
            P(None, "freq", "param", None),
            P("freq", None),
            P("freq", None),
            P("freq"),
        ),
        out_specs=(P("freq", "param", None), P("freq", "param", None)),
        check_vma=False,
    )
```

time: 80.6 us -> 72.6 us (0.901)
  Pallas kernels: 76.3 us -> 70.9 us
  local copies, waits for them, and re-layouts: 2.85 us -> 0.2 us
    pallas_call x1, Pallas kernels: 70.5 us -> 65.8 us  [kernel_steps(): pl.pallas_call(functools.partial(steps_kernel, freq_count, param_count, C...]
    unnamed x10 -> x2, local copies, waits for them, and re-layouts: 2.66 us -> 0.01 us
where the time goes in v3:
time: 72.6 us; the launch traced here: 72.4 us
  Pallas kernels  70.9 us (98%)
    pallas_call x1, Pallas kernels, kernel_steps(): pl.pallas_call(functools.partial(steps_kernel, freq_count, param_count, C...  65.8 us
    pallas_call x1, Pallas kernels, kernel_steps(): pl.pallas_call(final_kernel, out_shape=[jax.ShapeDtypeStruct(chain_state....  5.09 us

profile of v3, /device:TPU:0, one launch (start us, length us, event | category | flops | bytes accessed | tf_op | source)
XLA Modules:
  0.0 72.4 jit_solution(109054346683219548)
XLA Ops:
  0.6 0.6 fusion.7
  1.3 0.1 copy.9
  1.4 0.1 convert_element_type.24
  1.5 0.0 copy-start
  1.5 65.8 %shard_map.86 = (bf16[4,4,16,8,256]{4,3,2,1,0:T(8,128)(2,1)S(1)}, f32[8,256,512]{2,1,0:T(8,128)S(1)}, f32[8,256,512]{2,1,0:T(8,128)S(1)}) custom-call(bf16[128,512]{1,0:T(8,128)(2,1)S(1)} %bitcast.3, f32[8]{0:T(128)} %temper_ref.1, f32[16,1024]{1,0:T(8,128)} %obs_hbm.1, f32[16,512]{1,0:T(8,128)} %inv_hbm.1, f32[8,256,512]{2,1,0:T(8,128)} %state_hbm.1, ...), custom_call_target="tpu_custom_call" | custom-call | tf_op jit(solution)/shard_map/pallas_call | solution.py:529
  67.3 0.0 copy-done
  67.3 5.1 %shard_map.87 = (f32[8,256,512]{2,1,0:T(8,128)}, f32[8,256,512]{2,1,0:T(8,128)}) custom-call(bf16[128,512]{1,0:T(8,128)(2,1)S(1)} %bitcast.4, f32[8]{0:T(128)S(1)} %copy-done, bf16[4,4,16,8,256]{4,3,2,1,0:T(8,128)(2,1)S(1)} %get-tuple-element.5.adj_all, f32[8,256,512]{2,1,0:T(8,128)S(1)} %get-tuple-element.6.state, ...), custom_call_target="tpu_custom_call" | custom-call | tf_op jit(solution)/shard_map/pallas_call | solution.py:569
  (2 shorter events, 0.0 us)
Async XLA Ops:
  1.5 65.8 %copy-start = (f32[8]{0:T(128)S(1)}, f32[8]{0:T(128)}, u32[]{:S(2)}) copy-start(f32[8]{0:T(128)} %temper_ref.1) | copy-start | bytes 100

commit v4 on v3

--- a/solution.py
+++ b/solution.py
@@ -19,6 +19,7 @@
 GATHER_LAG = 3
 ADJ_LAG = 8
 SPEC_LAG = 9
+TABLE_ROWS = 16
 
 
 def spectral_table(time_len, freq_total):
@@ -35,11 +36,11 @@
 
 def steps_kernel(
     freq_count, param_count, chunk_freqs,
-    table_ref, temper_hbm, obs_hbm, inv_hbm, state_hbm, moment_hbm, noise_hbm, green_hbm,
-    adj_all, state, moment,
+    temper_hbm, obs_hbm, inv_hbm, state_hbm, moment_hbm, noise_hbm, green_hbm,
+    adj_all, state, moment, push, table_ref,
     temper_ref, obs_all, inv_all, obs_rows, inv_rows, green, noise, rows32, spec, field, acc,
     core_out, core_in, up_out, up_in, down_out, down_in, wtd, adj,
-    small_sem, state_sem, green_sem, moment_sem, noise_sem, spec_send, spec_recv,
+    small_sem, state_sem, green_sem, moment_sem, noise_sem, push_sem, spec_send, spec_recv,
     line_send, line_recv, adj_send, adj_recv,
 ):
     freq_me = lax.axis_index("freq")
@@ -90,6 +91,10 @@
     def noise_copy(s, c):
         return pltpu.make_async_copy(noise_hbm.at[s, c], noise.at[s, c], noise_sem.at[s])
 
+    def push_copy():
+        left = pl.ds((groups - 1) * group_chains, group_chains)
+        return pltpu.make_async_copy(noise_hbm.at[steps - 1, left], push, push_sem.at[0])
+
     def small_copy(k, src, dst):
         return pltpu.make_async_copy(src, dst, small_sem.at[k])
 
@@ -164,7 +169,7 @@
             for d in range(1, freq_count):
                 spec_copy(q, g, i, d).start()
 
-    @pl.loop(0, groups * group_chains)
+    @pl.loop(0, group_chains)
     def _(c):
         state_copy(c).start()
 
@@ -172,12 +177,15 @@
     for k, (src, dst) in enumerate(smalls):
         small_copy(k, src, dst).start()
 
+    fill_table(table_ref)
     met = has_above.astype(jnp.int32) + has_below.astype(jnp.int32)
     for g in range(groups):
         @pl.loop(0, group_chains)
         def _(k):
             c = g * group_chains + k
             state_copy(c).wait()
+            if g < groups - 1:
+                state_copy(c + group_chains).start()
             transform(g, k, state[c].astype(jnp.bfloat16))
 
         if g == groups - 1:
@@ -188,8 +196,14 @@
             @pl.loop(0, groups * group_chains)
             def _(c):
                 moment_copy(c).start()
-                for s in range(steps):
+                for s in range(steps - 1):
                     noise_copy(s, c).start()
+
+            @pl.loop(0, (groups - 1) * group_chains)
+            def _(c):
+                noise_copy(steps - 1, c).start()
+
+            push_copy().start()
 
         if g == 0:
             pl.semaphore_wait(barrier, freq_count + met)
@@ -331,7 +345,14 @@
                     def _():
                         arrived(moment, moment_sem.at[0])
 
-                    arrived(noise.at[s], noise_sem.at[s])
+                    @pl.when(going_on)
+                    def _():
+                        arrived(noise.at[s], noise_sem.at[s])
+
+                    @pl.when(s == steps - 1)
+                    def _():
+                        read = pl.ds(0, (groups - 1) * group_chains)
+                        arrived(noise.at[s, read], noise_sem.at[s])
 
             c = g * group_chains + k
             low = advance(
@@ -379,6 +400,7 @@
         stage(update_lag, update)
 
     last = steps * groups - 1
+    push_copy().wait()
     arrived(adj_all.at[last, peers], adj_recv.at[groups - 1])
     arrived(spec.at[:, peers], spec_send.at[0])
     arrived(adj.at[:, :, peers], adj_send.at[0])
@@ -392,6 +414,20 @@
     @pl.when(has_below)
     def _():
         arrived(core_out, line_send.at[3])
+
+
+def fill_table(table_ref):
+    columns, time_len = table_ref.shape
+
+    @pl.loop(0, columns // TABLE_ROWS)
+    def _(i):
+        first = pl.multiple_of(i * TABLE_ROWS, TABLE_ROWS)
+        column = lax.broadcasted_iota(jnp.int32, (TABLE_ROWS, time_len), 0) + first
+        time_index = lax.broadcasted_iota(jnp.int32, (TABLE_ROWS, time_len), 1)
+        turn = time_index * ((column >> 1) + 1) + (column & 1) * (time_len // 4)
+        phase_angle = (turn & (time_len - 1)).astype(jnp.float32) * (2.0 * math.pi / time_len)
+        rows = jnp.cos(phase_angle) / math.sqrt(time_len)
+        table_ref[pl.ds(first, TABLE_ROWS)] = rows.astype(jnp.bfloat16)
 
 
 def widen(adj, rows32):
@@ -430,15 +466,12 @@
 
 
 def final_kernel(
-    table_ref, temper_ref, adj_all, state, moment, noise_hbm, state_hbm, moment_hbm,
-    rows32, push, new_state, new_moment, push_sem, state_sem, moment_sem,
+    table_ref, temper_ref, adj_all, state, moment, push, state_hbm, moment_hbm,
+    rows32, new_state, new_moment, state_sem, moment_sem,
 ):
-    last, step = adj_all.shape[0] - 1, noise_hbm.shape[0] - 1
+    last = adj_all.shape[0] - 1
     left = new_state.shape[0]
     done = state.shape[0] - left
-
-    def push_copy(k):
-        return pltpu.make_async_copy(noise_hbm.at[step, done + k], push.at[k], push_sem.at[k])
 
     def state_copy(k):
         c = done + k
@@ -453,10 +486,6 @@
 
     def done_moment_copy(c):
         return pltpu.make_async_copy(moment.at[c], moment_hbm.at[c], moment_sem.at[c])
-
-    @pl.loop(0, left)
-    def _(k):
-        push_copy(k).start()
 
     @pl.loop(0, done)
     def _(c):
@@ -467,10 +496,10 @@
 
     @pl.loop(0, left)
     def _(k):
-        push_copy(k).wait()
+        here = pl.ds(done, left)
         advance(
-            k, k, rows32, table_ref, temper_ref.at[pl.ds(done, left)], state.at[pl.ds(done, left)],
-            moment.at[pl.ds(done, left)], push, new_state, new_moment,
+            k, k, rows32, table_ref, temper_ref.at[here], state.at[here], moment.at[here],
+            push, new_state, new_moment,
         )
         state_copy(k).start()
         moment_copy(k).start()
@@ -494,6 +523,8 @@
         and 2 * (chains_loc // GROUPS) % 8 == 0
         and slab % LANES == 0
         and chain_shape[2] % LANES == 0
+        and chain_shape[2] & (chain_shape[2] - 1) == 0
+        and 2 * green_shape[1] * lax.axis_size("freq") % TABLE_ROWS == 0
         and green_shape[3] % (2 * LANES) == 0
         and green_shape[1] % CHUNK_FREQS == 0
         and green_shape[1] // CHUNK_FREQS >= chains_loc // GROUPS
@@ -508,7 +539,6 @@
     steps = noise.shape[0]
     freq_count, param_count = lax.axis_size("freq"), lax.axis_size("param")
     columns = 2 * freq_loc * freq_count
-    table = spectral_table(time_len, freq_loc * freq_count).T
     chunks = freq_loc // CHUNK_FREQS
     group_chains = chains_loc // GROUPS
     rows, half = 2 * group_chains, sensors // 2
@@ -522,19 +552,21 @@
     line_buf = pltpu.VMEM((items, freq_loc, all_rows, half), bf16)
     rows32 = (slab // LANES, columns * group_chains, LANES)
     part = (group_chains, slab, time_len)
-    observed, inv_noise, temper_hbm, noise = (
+    operands = [
         pltpu.with_memory_space_constraint(x, pltpu.HBM)
-        for x in (observed, inv_noise, temper, noise)
-    )
-    adj_all, state, moment = pl.pallas_call(
+        for x in (temper, observed, inv_noise, chain_state, second_moment, noise, green)
+    ]
+    adj_all, state, moment, push, table = pl.pallas_call(
         functools.partial(steps_kernel, freq_count, param_count, CHUNK_FREQS),
         out_shape=[
             jax.ShapeDtypeStruct((items, freq_count, freq_loc, rows, slab), bf16),
             jax.ShapeDtypeStruct(chain_state.shape, f32),
             jax.ShapeDtypeStruct(chain_state.shape, f32),
+            jax.ShapeDtypeStruct(part, f32),
+            jax.ShapeDtypeStruct((columns, time_len), bf16),
         ],
-        in_specs=[vmem, hbm, hbm, hbm, hbm, hbm, hbm, hbm],
-        out_specs=[vmem, vmem, vmem],
+        in_specs=[hbm, hbm, hbm, hbm, hbm, hbm, hbm],
+        out_specs=[vmem, vmem, vmem, vmem, vmem],
         scratch_shapes=[
             pltpu.SMEM(temper.shape, f32),
             pltpu.VMEM(observed.shape, f32),
@@ -556,6 +588,7 @@
             dma((1,)),
             dma((steps,)),
             dma((1,)),
+            dma((1,)),
             dma((GROUPS, chunks)),
             dma((4,)),
             dma((4, GROUPS, chunks)),
@@ -563,28 +596,26 @@
             dma((GROUPS,)),
         ],
         compiler_params=pltpu.CompilerParams(
-            collective_id=0, has_side_effects=True, vmem_limit_bytes=44 * 2**20
+            collective_id=0, has_side_effects=True, vmem_limit_bytes=36 * 2**20
         ),
-    )(table, temper_hbm, observed, inv_noise, chain_state, second_moment, noise, green)
+    )(*operands)
     return pl.pallas_call(
         final_kernel,
         out_shape=[
             jax.ShapeDtypeStruct(chain_state.shape, f32),
             jax.ShapeDtypeStruct(chain_state.shape, f32),
         ],
-        in_specs=[vmem, smem, vmem, vmem, vmem, hbm],
+        in_specs=[vmem, smem, vmem, vmem, vmem, vmem],
         out_specs=[hbm, hbm],
         scratch_shapes=[
             pltpu.VMEM(rows32, f32),
             pltpu.VMEM(part, f32),
             pltpu.VMEM(part, f32),
-            pltpu.VMEM(part, f32),
-            dma((group_chains,)),
             dma((chains_loc,)),
             dma((chains_loc,)),
         ],
-        compiler_params=pltpu.CompilerParams(vmem_limit_bytes=18 * 2**20),
-    )(table, temper, adj_all, state, moment, noise)
+        compiler_params=pltpu.CompilerParams(vmem_limit_bytes=8 * 2**20),
+    )(table, temper, adj_all, state, moment, push)
 
 
 def on_device(chain_state, second_moment, noise, green, observed, inv_noise, temper):

time: 72.6 us -> 70.6 us (0.972)
  Pallas kernels: 70.9 us -> 69.8 us
    pallas_call x1, Pallas kernels: 5.09 us -> 3.96 us  [kernel_steps(): pl.pallas_call(final_kernel, out_shape=[jax.ShapeDtypeStruct(chain_state....]
where the time goes in v4:
time: 70.6 us; the launch traced here: 70.5 us
  Pallas kernels  69.8 us (99%)
    pallas_call x1, Pallas kernels, kernel_steps(): pl.pallas_call(functools.partial(steps_kernel, freq_count, param_count, C...  65.8 us
    pallas_call x1, Pallas kernels, kernel_steps(): pl.pallas_call(final_kernel, out_shape=[jax.ShapeDtypeStruct(chain_state....  3.96 us

profile of v4, /device:TPU:0, one launch (start us, length us, event | category | flops | bytes accessed | tf_op | source)
XLA Modules:
  0.0 70.5 jit_solution(11362738441618982895)
XLA Ops:
  0.6 0.0 copy-start
  0.6 65.8 %shard_map.86 = (bf16[4,4,16,8,256]{4,3,2,1,0:T(8,128)(2,1)S(1)}, f32[8,256,512]{2,1,0:T(8,128)S(1)}, f32[8,256,512]{2,1,0:T(8,128)S(1)}, f32[4,256,512]{2,1,0:T(8,128)S(1)}, bf16[128,512]{1,0:T(8,128)(2,1)S(1)}) custom-call(f32[8]{0:T(128)} %temper_ref.1, f32[16,1024]{1,0:T(8,128)} %obs_hbm.1, f32[16,512]{1,0:T(8,128)} %inv_hbm.1, ...), custom_call_target="tpu_custom_call" | custom-call | tf_op jit(solution)/shard_map/pallas_call | solution.py:559
  66.5 0.0 copy-done
  66.5 4.0 %shard_map.87 = (f32[8,256,512]{2,1,0:T(8,128)}, f32[8,256,512]{2,1,0:T(8,128)}) custom-call(bf16[128,512]{1,0:T(8,128)(2,1)S(1)} %get-tuple-element.7.table_ref, f32[8]{0:T(128)S(1)} %copy-done, bf16[4,4,16,8,256]{4,3,2,1,0:T(8,128)(2,1)S(1)} %get-tuple-element.8.adj_all, f32[8,256,512]{2,1,0:T(8,128)S(1)} %get-tuple-element.9.state, ...), custom_call_target="tpu_custom_call" | custom-call | tf_op jit(solution)/shard_map/pallas_call | solution.py:602
Async XLA Ops:
  0.6 65.9 %copy-start = (f32[8]{0:T(128)S(1)}, f32[8]{0:T(128)}, u32[]{:S(2)}) copy-start(f32[8]{0:T(128)} %temper_ref.1) | copy-start | bytes 100

commit v5 on v4

--- a/solution.py
+++ b/solution.py
@@ -20,6 +20,8 @@
 ADJ_LAG = 8
 SPEC_LAG = 9
 TABLE_ROWS = 16
+UPDATE_CHAINS = 4
+FINAL_CHAINS = 2
 
 
 def spectral_table(time_len, freq_total):
@@ -55,6 +57,7 @@
     col_blocks = slab // LANES
     columns = table_ref.shape[0]
     chunks = freq_loc // chunk_freqs
+    turns = group_chains // UPDATE_CHAINS
     line = param_count // 2
     core = lax.rem(param_me, 2)
     chip = param_me // 2
@@ -332,7 +335,7 @@
         q = s * groups + g
         going_on = s < steps - 1
 
-        @pl.when((k < group_chains) & (going_on | (g < groups - 1)))
+        @pl.when((k < turns) & (going_on | (g < groups - 1)))
         def _():
             @pl.when(k == 0)
             def _():
@@ -354,16 +357,21 @@
                         read = pl.ds(0, (groups - 1) * group_chains)
                         arrived(noise.at[s, read], noise_sem.at[s])
 
-            c = g * group_chains + k
-            low = advance(
-                k, c, rows32.at[g], table_ref, temper_ref, state, moment, noise.at[s], state, moment
-            )
+            lows = []
+            for e in range(UPDATE_CHAINS):
+                here = k * UPDATE_CHAINS + e
+                low = advance(
+                    here, g * group_chains + here, rows32.at[g], table_ref, temper_ref,
+                    state, moment, noise.at[s], state, moment,
+                )
+                lows.append(low)
 
             @pl.when(going_on)
             def _():
-                transform(g, k, low)
-
-            @pl.when(going_on & (k == group_chains - 1))
+                for e in range(UPDATE_CHAINS):
+                    transform(g, k * UPDATE_CHAINS + e, lows[e])
+
+            @pl.when(going_on & (k == turns - 1))
             def _():
                 send_spectrum(q + groups, g)
 
@@ -373,10 +381,10 @@
     weigh_lag = jnp.maximum(up_lag, down_lag)
     back_lag = CORE_LAG + HOP_LAG * (line - 1) + GATHER_LAG
     update_lag = back_lag + chunks - 1 + ADJ_LAG
-    period = max(update_lag + group_chains - 1 + SPEC_LAG, span)
+    period = max(update_lag + turns - 1 + SPEC_LAG, span)
     inside = has_above & has_below
     total_ticks = (steps - 1) * period + max(
-        span + back_lag, update_lag + (groups - 2) * chunks + group_chains
+        span + back_lag, update_lag + (groups - 2) * chunks + turns
     )
 
     @pl.loop(0, total_ticks)
@@ -454,12 +462,8 @@
     spread = moment[c]
     spread = decay_rate * spread + (1.0 - decay_rate) * drift_term * drift_term
     precondition = lax.rsqrt(spread)
-    root = precondition * lax.rsqrt(precondition)
-    current = (
-        current
-        - step_length * precondition * drift_term
-        + math.sqrt(2.0 * step_length) * root * push[c]
-    )
+    kick = math.sqrt(2.0 * step_length) * lax.rsqrt(precondition) * push[c]
+    current = current - precondition * (step_length * drift_term - kick)
     new_state[c] = current
     new_moment[c] = spread
     return current.astype(jnp.bfloat16)
@@ -494,15 +498,17 @@
 
     widen(adj_all.at[last], rows32)
 
-    @pl.loop(0, left)
-    def _(k):
+    @pl.loop(0, left // FINAL_CHAINS)
+    def _(i):
         here = pl.ds(done, left)
-        advance(
-            k, k, rows32, table_ref, temper_ref.at[here], state.at[here], moment.at[here],
-            push, new_state, new_moment,
-        )
-        state_copy(k).start()
-        moment_copy(k).start()
+        for e in range(FINAL_CHAINS):
+            k = i * FINAL_CHAINS + e
+            advance(
+                k, k, rows32, table_ref, temper_ref.at[here], state.at[here], moment.at[here],
+                push, new_state, new_moment,
+            )
+            state_copy(k).start()
+            moment_copy(k).start()
 
     @pl.loop(0, done)
     def _(c):
@@ -528,6 +534,8 @@
         and green_shape[3] % (2 * LANES) == 0
         and green_shape[1] % CHUNK_FREQS == 0
         and green_shape[1] // CHUNK_FREQS >= chains_loc // GROUPS
+        and chains_loc // GROUPS % UPDATE_CHAINS == 0
+        and chains_loc // GROUPS % FINAL_CHAINS == 0
         and param_count == 8
         and lax.axis_size("freq") > 1
     )

time: 70.6 us -> 69 us (0.977)
  Pallas kernels: 69.8 us -> 68.2 us
    pallas_call x1, Pallas kernels: 65.8 us -> 64.2 us  [kernel_steps(): pl.pallas_call(functools.partial(steps_kernel, freq_count, param_count, C...]
where the time goes in v5:
time: 69 us; the launch traced here: 68.8 us
  Pallas kernels  68.2 us (99%)
    pallas_call x1, Pallas kernels, kernel_steps(): pl.pallas_call(functools.partial(steps_kernel, freq_count, param_count, C...  64.2 us
    pallas_call x1, Pallas kernels, kernel_steps(): pl.pallas_call(final_kernel, out_shape=[jax.ShapeDtypeStruct(chain_state....  3.96 us

profile of v5, /device:TPU:0, one launch (start us, length us, event | category | flops | bytes accessed | tf_op | source)
XLA Modules:
  0.0 68.8 jit_solution(3182519250881095814)
XLA Ops:
  0.6 0.0 copy-start
  0.6 64.2 %shard_map.86 = (bf16[4,4,16,8,256]{4,3,2,1,0:T(8,128)(2,1)S(1)}, f32[8,256,512]{2,1,0:T(8,128)S(1)}, f32[8,256,512]{2,1,0:T(8,128)S(1)}, f32[4,256,512]{2,1,0:T(8,128)S(1)}, bf16[128,512]{1,0:T(8,128)(2,1)S(1)}) custom-call(f32[8]{0:T(128)} %temper_ref.1, f32[16,1024]{1,0:T(8,128)} %obs_hbm.1, f32[16,512]{1,0:T(8,128)} %inv_hbm.1, ...), custom_call_target="tpu_custom_call" | custom-call | tf_op jit(solution)/shard_map/pallas_call | solution.py:567
  64.9 0.0 copy-done
  64.9 4.0 %shard_map.87 = (f32[8,256,512]{2,1,0:T(8,128)}, f32[8,256,512]{2,1,0:T(8,128)}) custom-call(bf16[128,512]{1,0:T(8,128)(2,1)S(1)} %get-tuple-element.7.table_ref, f32[8]{0:T(128)S(1)} %copy-done, bf16[4,4,16,8,256]{4,3,2,1,0:T(8,128)(2,1)S(1)} %get-tuple-element.8.adj_all, f32[8,256,512]{2,1,0:T(8,128)S(1)} %get-tuple-element.9.state, ...), custom_call_target="tpu_custom_call" | custom-call | tf_op jit(solution)/shard_map/pallas_call | solution.py:610
Async XLA Ops:
  0.6 64.2 %copy-start = (f32[8]{0:T(128)S(1)}, f32[8]{0:T(128)}, u32[]{:S(2)}) copy-start(f32[8]{0:T(128)} %temper_ref.1) | copy-start | bytes 100
